TPU v7x, 768 devices: a whole 4x8x12 slice. The times are simulated.
768 devices in a mesh: gx: 8 (over x, core), gy: 12 (over z), gz: 8 (over y).
Axes of the slice: x: 4, y: 8, z: 12, core: 2. Of those that a mesh axis runs over, the one named last changes fastest.
Arguments:
- fine_blocks: float32 [16, 24, 32, 7, 4096], P('gx', 'gy', 'gz'), may hold values from -0.75 to 0.75
- prolong: float32 [16, 24, 32, 1024], P('gx', 'gy', 'gz'), may hold values from -1.5 to 1.5
- agg_map: int32 [16, 24, 32], replicated, may hold values from 0 to 7, as said below
- owner_map: int32 [8, 12, 64], P('gx', 'gy', 'gz'), may hold values from 0 to 7, as said below
Outputs:
- coarse_rows: float32 [8, 12, 64, 14336], P('gx', 'gy', 'gz')
Inputs may be any that keep to these rules, and one draw needn't show every extreme that they name: `agg_map`: every one of the 8 slots of each brick names at least one element of that brick. `owner_map`: owners are devices with the same gx and gy indices as the brick. Each brick gives exactly 1 of its slots to each owner. The elements of one brick whose rows go to one owner number at most 4, and exactly 4 for one owner of every brick.
All inputs are finite; a program needn't handle non-finite values.
Results may differ from a plain program's by a relative error of at most 0.0001.
Values sent between devices are 32-bit elements; how exact they have to be, the bound alone decides.
A program may use at most 32 MiB of HBM per device.

v0:
```python
import jax
import jax.numpy as jnp
from jax import lax
from jax.sharding import PartitionSpec as P

DOF = 64
CDOF = 16
AGGS = 8


face_steps = ((0, 0, 0), (-1, 0, 0), (1, 0, 0), (0, -1, 0), (0, 1, 0), (0, 0, -1), (0, 0, 1))


def extended(block, sides, width):
    for axis, dim in sides:
        count = lax.axis_size(axis)
        forward = [(i, i + 1) for i in range(count - 1)]
        backward = [(target, source) for source, target in forward]
        low = lax.ppermute(
            lax.slice_in_dim(block, block.shape[dim] - width, None, axis=dim), axis, forward
        )
        high = lax.ppermute(lax.slice_in_dim(block, 0, width, axis=dim), axis, backward)
        block = jnp.concatenate([low, block, high], axis=dim)
    return block


def shards(fine_blocks, prolong, agg_map, owner_map):
    size_x = fine_blocks.shape[0]
    size_y = fine_blocks.shape[1]
    size_z = fine_blocks.shape[2]
    elements = size_x * size_y * size_z
    group_size = lax.axis_size("gz")
    rows_each = AGGS // group_size
    capacity = min(2 * elements // group_size, elements - (group_size - 1) * rows_each)
    padded = extended(prolong, (("gx", 0), ("gy", 1), ("gz", 2)), 1)
    window = padded.reshape(size_x + 2, size_y + 2, size_z + 2, DOF, CDOF)
    beside = jnp.stack(
        [
            window[1 + sx : 1 + sx + size_x, 1 + sy : 1 + sy + size_y, 1 + sz : 1 + sz + size_z]
            for sx, sy, sz in face_steps
        ],
        axis=3,
    )
    blocks = fine_blocks.reshape(size_x, size_y, size_z, 7, DOF, DOF)
    products = jnp.einsum("xyzkij,xyzkjc->xyzkic", blocks, beside, precision=lax.Precision.HIGHEST)
    own_base = window[1:-1, 1:-1, 1:-1]
    anchor_x = lax.axis_index("gx") * size_x
    anchor_y = lax.axis_index("gy") * size_y
    anchor_z = lax.axis_index("gz") * size_z
    padded_agg = jnp.pad(agg_map, 1)
    agg_window = lax.dynamic_slice(
        padded_agg, (anchor_x, anchor_y, anchor_z), (size_x + 2, size_y + 2, size_z + 2)
    )
    local_x = jnp.arange(size_x, dtype=jnp.int32)[:, None, None]
    local_y = jnp.arange(size_y, dtype=jnp.int32)[None, :, None]
    local_z = jnp.arange(size_z, dtype=jnp.int32)[None, None, :]
    columns = []
    for face, (sx, sy, sz) in enumerate(face_steps):
        neighbour = agg_window[
            1 + sx : 1 + sx + size_x, 1 + sy : 1 + sy + size_y, 1 + sz : 1 + sz + size_z
        ]
        inside = (
            (local_x + sx >= 0)
            & (local_x + sx < size_x)
            & (local_y + sy >= 0)
            & (local_y + sy < size_y)
            & (local_z + sz >= 0)
            & (local_z + sz < size_z)
        )
        relation = jnp.where(inside, 0, face).astype(jnp.int32)
        columns.append(relation * AGGS + neighbour)
    column_slot = jnp.stack(columns, axis=3).reshape(elements, 7)
    own_agg = agg_window[1:-1, 1:-1, 1:-1].reshape(elements)
    owners = owner_map.reshape(AGGS)
    slot_ids = jnp.arange(AGGS, dtype=jnp.int32)
    earlier = (owners[None, :] == owners[:, None]) & (slot_ids[None, :] < slot_ids[:, None])
    rank_in_owner = jnp.sum(earlier.astype(jnp.int32), axis=1)
    member = (own_agg[:, None] == slot_ids[None, :]).astype(jnp.int32)
    element_owner = jnp.sum(member * owners[None, :], axis=1)
    element_rank = jnp.sum(member * rank_in_owner[None, :], axis=1)
    element_ids = jnp.arange(elements, dtype=jnp.int32)
    before = (element_owner[None, :] == element_owner[:, None]) & (
        element_ids[None, :] < element_ids[:, None]
    )
    position = jnp.sum(before.astype(jnp.int32), axis=1)
    owner_ids = jnp.arange(group_size, dtype=jnp.int32)
    place_ids = jnp.arange(capacity, dtype=jnp.int32)
    select = (
        (element_owner[None, None, :] == owner_ids[:, None, None])
        & (position[None, None, :] == place_ids[None, :, None])
    ).astype(jnp.float32)
    labels = jnp.concatenate([element_rank[:, None], column_slot], axis=1).astype(jnp.float32)

    def bucket(values):
        return jnp.einsum("oce,ef->ocf", select, values, precision=lax.Precision.HIGHEST)

    coarse = jnp.einsum("xyzic,xyzkid->xyzkcd", own_base, products, precision=lax.Precision.HIGHEST)
    received, received_labels = (
        lax.all_to_all(
            bucket(coarse.reshape(elements, 7 * CDOF * CDOF)),
            "gz",
            split_axis=0,
            concat_axis=0,
            tiled=True,
        ),
        lax.all_to_all(bucket(labels), "gz", split_axis=0, concat_axis=0, tiled=True),
    )
    sender_ids = jnp.arange(group_size, dtype=jnp.float32)[:, None]
    row_target = sender_ids * rows_each + received_labels[:, :, 0]
    target = row_target[:, :, None] * (7 * AGGS) + received_labels[:, :, 1:]
    target_ids = jnp.arange(AGGS * 7 * AGGS, dtype=jnp.float32)
    spread = (target.reshape(group_size * capacity * 7)[:, None] == target_ids[None, :]).astype(
        jnp.float32
    )
    flat_terms = received.reshape(group_size * capacity * 7, CDOF * CDOF)
    summed = jnp.einsum("rm,rf->mf", spread, flat_terms, precision=lax.Precision.HIGHEST)
    return summed.reshape(1, 1, AGGS, 7 * AGGS * CDOF * CDOF)


def solution(mesh):
    placed = (P("gx", "gy", "gz", None, None), P("gx", "gy", "gz", None), P(), P("gx", "gy", "gz"))
    return jax.shard_map(
        shards, mesh=mesh, in_specs=placed, out_specs=P("gx", "gy", "gz", None), check_vma=False
    )
```

profile of v0, /device:TPU:194, one launch (start us, length us, event | category | flops | bytes accessed | tf_op | source)
XLA Modules:
  0.0 98.4 jit_solution(7837936637338704260)
XLA Ops:
  0.8 1.9 %collective-permute-start = (f32[1,2,4,1024]{3,2,1,0:T(4,128)S(1)}, f32[1,2,4,1024]{3,2,1,0:T(4,128)S(1)}, u32[]{:S(2)}, u32[]{:S(2)}) collective-permute-start(f32[1,2,4,1024]{3,2,1,0:T(4,128)S(1)} %get-tuple-element.26), channel_id=1, source_target_pairs={{0,96},{96,192},{192,288},{288,384},{384,480},{480,576},{576,672},... | collective-permute-start | bytes 98312 | tf_op jit(solution)/shard_map/ppermute | solution.py:19
  2.7 3.6 %collective-permute-start.1 = (f32[1,2,4,1024]{3,2,1,0:T(4,128)S(1)}, f32[1,2,4,1024]{3,2,1,0:T(4,128)S(1)}, u32[]{:S(2)}, u32[]{:S(2)}) collective-permute-start(f32[1,2,4,1024]{3,2,1,0:T(4,128)S(1)} %get-tuple-element.25), channel_id=1, source_target_pairs={{96,0},{192,96},{288,192},{384,288},{480,384},{576,480},{672,576},... | collective-permute-start | bytes 98312 | tf_op jit(solution)/shard_map/ppermute | solution.py:22
  11.3 5.5 %collective-permute-start.2 = (f32[4,1,4,1024]{3,2,1,0:T(4,128)S(1)}, f32[4,1,4,1024]{3,2,1,0:T(4,128)S(1)}, u32[]{:S(2)}, u32[]{:S(2)}) collective-permute-start(f32[4,1,4,1024]{3,2,1,0:T(4,128)S(1)} %get-tuple-element.23), channel_id=1, source_target_pairs={{0,8},{8,16},{16,24},{24,32},{32,40},{40,48},{48,56},{56,64},{64,7... | collective-permute-start | bytes 196616 | tf_op jit(solution)/shard_map/ppermute | solution.py:19
  16.8 1.9 %collective-permute-start.3 = (f32[4,1,4,1024]{3,2,1,0:T(4,128)S(1)}, f32[4,1,4,1024]{3,2,1,0:T(4,128)S(1)}, u32[]{:S(2)}, u32[]{:S(2)}) collective-permute-start(f32[4,1,4,1024]{3,2,1,0:T(4,128)S(1)} %get-tuple-element.24), channel_id=1, source_target_pairs={{8,0},{16,8},{24,16},{32,24},{40,32},{48,40},{56,48},{64,56},{72,6... | collective-permute-start | bytes 196616 | tf_op jit(solution)/shard_map/ppermute | solution.py:22
  19.4 4.8 %collective-permute-done.3 = f32[4,1,4,1024]{3,2,1,0:T(4,128)S(1)} collective-permute-done((f32[4,1,4,1024]{3,2,1,0:T(4,128)S(1)}, f32[4,1,4,1024]{3,2,1,0:T(4,128)S(1)}, u32[]{:S(2)}, u32[]{:S(2)}) %collective-permute-start.3) | collective-permute-done | bytes 65568 | tf_op jit(solution)/shard_map/ppermute | solution.py:22
  24.3 3.5 %collective-permute-start.4 = (f32[4,4,1,1024]{3,2,1,0:T(1,128)S(1)}, f32[4,4,1,1024]{3,2,1,0:T(1,128)S(1)}, u32[]{:S(2)}, u32[]{:S(2)}) collective-permute-start(f32[4,4,1,1024]{3,2,1,0:T(1,128)S(1)} %get-tuple-element.14), channel_id=1, source_target_pairs={{0,1},{1,2},{2,3},{3,4},{4,5},{5,6},{6,7},{8,9},{9,10},{10,11},{11... | collective-permute-start | bytes 196616 | tf_op jit(solution)/shard_map/ppermute | solution.py:19
  27.8 1.3 %collective-permute-start.5 = (f32[4,4,1,1024]{3,2,1,0:T(1,128)S(1)}, f32[4,4,1,1024]{3,2,1,0:T(1,128)S(1)}, u32[]{:S(2)}, u32[]{:S(2)}) collective-permute-start(f32[4,4,1,1024]{3,2,1,0:T(1,128)S(1)} %get-tuple-element.15), channel_id=1, source_target_pairs={{1,0},{2,1},{3,2},{4,3},{5,4},{6,5},{7,6},{9,8},{10,9},{11,10},{12... | collective-permute-start | bytes 196616 | tf_op jit(solution)/shard_map/ppermute | solution.py:22
  29.8 9.4 %all-to-all-start = ((f32[8,4,8]{2,1,0:T(4,128)}), f32[8,4,8]{2,1,0:T(4,128)S(1)}, u32[]{:S(2)}, u32[]{:S(2)}) async-start(f32[8,4,8]{2,1,0:T(4,128)} %fusion.10), calls=%async_computation | async-start | bytes 32768 | tf_op jit(solution)/shard_map/all_to_all | solution.py:106
  39.2 4.4 %reshape.364 = f32[2,2,4,7,64,64]{5,4,2,3,1,0:T(8,128)} reshape(f32[2,2,4,7,4096]{4,2,3,1,0:T(4,128)} %param.4) | data formatting | bytes 3670016 | tf_op jit(solution)/shard_map/reshape | solution.py:44
  43.6 3.4 %all-to-all-done = f32[8,4,8]{2,1,0:T(4,128)S(1)} async-done(((f32[8,4,8]{2,1,0:T(4,128)}), f32[8,4,8]{2,1,0:T(4,128)S(1)}, u32[]{:S(2)}, u32[]{:S(2)}) %all-to-all-start) | async-done | bytes 1056 | tf_op jit(solution)/shard_map/all_to_all | solution.py:106
  48.6 2.1 %reshape.372 = f32[4,4,6,64,16]{4,3,2,1,0:T(8,128)S(1)} reshape(f32[4,4,6,1024]{3,2,1,0:T(8,128)} %pad_maximum_fusion) | data formatting | bytes 786432 | tf_op jit(solution)/shard_map/reshape | solution.py:36
  50.7 1.9 %fusion.39 = (f32[2,2,4,64,16]{4,3,2,1,0:T(8,128)}, f32[2,2,4,64,16]{4,3,2,1,0:T(8,128)}, f32[2,2,4,64,16]{4,3,2,1,0:T(8,128)}, f32[2,2,4,64,16]{4,3,2,1,0:T(8,1...) fusion(f32[4,4,6,64,16]{4,3,2,1,0:T(8,128)S(1)} %reshape.372), kind=kLoop, calls=%fused_computation.89 | loop fusion | bytes 917504 | tf_op jit(solution)/shard_map/slice | solution.py:39
  54.5 1.9 %copy.66 = f32[2,2,4,64,16]{3,4,2,1,0:T(8,128)} copy(f32[2,2,4,64,16]{4,3,2,1,0:T(8,128)} %get-tuple-element.12) | data formatting | bytes 131072
  56.4 1.9 %copy.67 = f32[2,2,4,64,16]{3,4,2,1,0:T(8,128)} copy(f32[2,2,4,64,16]{4,3,2,1,0:T(8,128)} %get-tuple-element.11) | data formatting | bytes 131072
  58.3 1.9 %copy.68 = f32[2,2,4,64,16]{3,4,2,1,0:T(8,128)} copy(f32[2,2,4,64,16]{4,3,2,1,0:T(8,128)} %get-tuple-element.10) | data formatting | bytes 131072
  61.4 1.2 %copy.70 = f32[2,2,4,64,16]{3,4,2,1,0:T(8,128)S(1)} copy(f32[2,2,4,64,16]{4,3,2,1,0:T(8,128)} %get-tuple-element.8) | data formatting | bytes 131072
  63.9 1.6 %bitcast_dynamic-update-slice_fusion.5 = f32[2,2,4,7,64,16]{4,5,3,2,1,0:T(8,128)} fusion(f32[2,2,4,7,64,16]{4,5,3,2,1,0:T(8,128)} %bitcast_dynamic-update-slice_fusion.6, f32[2,2,4,64,16]{3,4,2,1,0:T(8,128)} %copy.66), kind=kLoop, calls=%fused_computation.21 | loop fusion | bytes 262144
  65.4 1.6 %bitcast_dynamic-update-slice_fusion.4 = f32[2,2,4,7,64,16]{4,5,3,2,1,0:T(8,128)} fusion(f32[2,2,4,7,64,16]{4,5,3,2,1,0:T(8,128)} %bitcast_dynamic-update-slice_fusion.5, f32[2,2,4,64,16]{3,4,2,1,0:T(8,128)} %copy.67), kind=kLoop, calls=%fused_computation.20 | loop fusion | bytes 262144
  67.0 1.6 %bitcast_dynamic-update-slice_fusion.3 = f32[2,2,4,7,64,16]{4,5,3,2,1,0:T(8,128)} fusion(f32[2,2,4,7,64,16]{4,5,3,2,1,0:T(8,128)} %bitcast_dynamic-update-slice_fusion.4, f32[2,2,4,64,16]{3,4,2,1,0:T(8,128)} %copy.68), kind=kLoop, calls=%fused_computation.19 | loop fusion | bytes 262144
  70.6 7.6 %fusion.2 = f32[2,2,4,7,64,16]{4,5,3,2,1,0:T(8,128)S(1)} fusion(f32[2,2,4,7,64,16]{4,5,3,2,1,0:T(8,128)} %bitcast_dynamic-update-slice_fusion, f32[2,2,4,7,64,64]{5,4,2,3,1,0:T(8,128)} %reshape.364), kind=kOutput, calls=%fused_computation.2 | convolution fusion | flops 88080384 | bytes 2752512 | tf_op jit(solution)/shard_map/xyzkij,xyzkjc->xyzkic/dot_general | solution.py:45
  78.2 1.9 %convolution_bitcast_fusion = f32[2,2,4,7,16,16]{4,5,3,2,1,0:T(8,128)} fusion(f32[2,2,4,7,64,16]{4,5,3,2,1,0:T(8,128)S(1)} %fusion.2, f32[4,4,6,64,16]{4,3,2,1,0:T(8,128)S(1)} %reshape.372), kind=kOutput, calls=%fused_computation.3 | convolution fusion | flops 22020096 | bytes 1556480 | tf_op jit(solution)/shard_map/xyzic,xyzkid->xyzkcd/dot_general | solution.py:97
  80.1 1.5 %copy.56 = f32[2,2,4,7,16,16]{5,4,3,2,1,0:T(8,128)S(1)} copy(f32[2,2,4,7,16,16]{4,5,3,2,1,0:T(8,128)} %convolution_bitcast_fusion) | data formatting | bytes 229376 | tf_op jit(solution)/shard_map/xyzic,xyzkid->xyzkcd/transpose | solution.py:97
  82.9 3.8 %all-to-all-start.1 = ((f32[8,4,1792]{2,1,0:T(4,128)}), f32[8,4,1792]{2,1,0:T(4,128)S(1)}, u32[]{:S(2)}, u32[]{:S(2)}) async-start(f32[8,4,1792]{2,1,0:T(4,128)} %fusion.8), calls=%async_computation.1 | async-start | bytes 458752 | tf_op jit(solution)/shard_map/all_to_all | solution.py:99
  87.0 9.8 %all-to-all-done.1 = f32[8,4,1792]{2,1,0:T(4,128)S(1)} async-done(((f32[8,4,1792]{2,1,0:T(4,128)}), f32[8,4,1792]{2,1,0:T(4,128)S(1)}, u32[]{:S(2)}, u32[]{:S(2)}) %all-to-all-start.1) | async-done | bytes 229408 | tf_op jit(solution)/shard_map/all_to_all | solution.py:99
  (61 shorter events, 18.4 us)
Async XLA Ops:
  0.8 9.6 %collective-permute-start = (f32[1,2,4,1024]{3,2,1,0:T(4,128)S(1)}, f32[1,2,4,1024]{3,2,1,0:T(4,128)S(1)}, u32[]{:S(2)}, u32[]{:S(2)}) collective-permute-start(f32[1,2,4,1024]{3,2,1,0:T(4,128)S(1)} %get-tuple-element.26), channel_id=1, source_target_pairs={{0,96},{96,192},{192,288},{288,384},{384,480},{480,576},{576,672},... | collective-permute-start | bytes 98312 | tf_op jit(solution)/shard_map/ppermute | solution.py:19
  2.7 8.6 %collective-permute-start.1 = (f32[1,2,4,1024]{3,2,1,0:T(4,128)S(1)}, f32[1,2,4,1024]{3,2,1,0:T(4,128)S(1)}, u32[]{:S(2)}, u32[]{:S(2)}) collective-permute-start(f32[1,2,4,1024]{3,2,1,0:T(4,128)S(1)} %get-tuple-element.25), channel_id=1, source_target_pairs={{96,0},{192,96},{288,192},{384,288},{480,384},{576,480},{672,576},... | collective-permute-start | bytes 98312 | tf_op jit(solution)/shard_map/ppermute | solution.py:22
  11.3 8.0 %collective-permute-start.2 = (f32[4,1,4,1024]{3,2,1,0:T(4,128)S(1)}, f32[4,1,4,1024]{3,2,1,0:T(4,128)S(1)}, u32[]{:S(2)}, u32[]{:S(2)}) collective-permute-start(f32[4,1,4,1024]{3,2,1,0:T(4,128)S(1)} %get-tuple-element.23), channel_id=1, source_target_pairs={{0,8},{8,16},{16,24},{24,32},{32,40},{40,48},{48,56},{56,64},{64,7... | collective-permute-start | bytes 196616 | tf_op jit(solution)/shard_map/ppermute | solution.py:19
  16.8 7.4 %collective-permute-start.3 = (f32[4,1,4,1024]{3,2,1,0:T(4,128)S(1)}, f32[4,1,4,1024]{3,2,1,0:T(4,128)S(1)}, u32[]{:S(2)}, u32[]{:S(2)}) collective-permute-start(f32[4,1,4,1024]{3,2,1,0:T(4,128)S(1)} %get-tuple-element.24), channel_id=1, source_target_pairs={{8,0},{16,8},{24,16},{32,24},{40,32},{48,40},{56,48},{64,56},{72,6... | collective-permute-start | bytes 196616 | tf_op jit(solution)/shard_map/ppermute | solution.py:22
  18.8 28.9 %copy-start = (pred[8,4,16]{2,0,1:T(8,128)(4,1)}, pred[8,4,16]{2,0,1:T(8,128)(4,1)S(1)}, u32[]{:S(2)}) copy-start(pred[8,4,16]{2,0,1:T(8,128)(4,1)S(1)} %broadcast_and_fusion) | copy-start | bytes 1540
  24.3 23.4 %collective-permute-start.4 = (f32[4,4,1,1024]{3,2,1,0:T(1,128)S(1)}, f32[4,4,1,1024]{3,2,1,0:T(1,128)S(1)}, u32[]{:S(2)}, u32[]{:S(2)}) collective-permute-start(f32[4,4,1,1024]{3,2,1,0:T(1,128)S(1)} %get-tuple-element.14), channel_id=1, source_target_pairs={{0,1},{1,2},{2,3},{3,4},{4,5},{5,6},{6,7},{8,9},{9,10},{10,11},{11... | collective-permute-start | bytes 196616 | tf_op jit(solution)/shard_map/ppermute | solution.py:19
  27.8 19.9 %collective-permute-start.5 = (f32[4,4,1,1024]{3,2,1,0:T(1,128)S(1)}, f32[4,4,1,1024]{3,2,1,0:T(1,128)S(1)}, u32[]{:S(2)}, u32[]{:S(2)}) collective-permute-start(f32[4,4,1,1024]{3,2,1,0:T(1,128)S(1)} %get-tuple-element.15), channel_id=1, source_target_pairs={{1,0},{2,1},{3,2},{4,3},{5,4},{6,5},{7,6},{9,8},{10,9},{11,10},{12... | collective-permute-start | bytes 196616 | tf_op jit(solution)/shard_map/ppermute | solution.py:22
  29.8 17.2 %all-to-all-start = ((f32[8,4,8]{2,1,0:T(4,128)}), f32[8,4,8]{2,1,0:T(4,128)S(1)}, u32[]{:S(2)}, u32[]{:S(2)}) async-start(f32[8,4,8]{2,1,0:T(4,128)} %fusion.10), calls=%async_computation | async-start | bytes 32768 | tf_op jit(solution)/shard_map/all_to_all | solution.py:106
  78.2 3.8 %copy-start.1 = (pred[8,4,16]{2,0,1:T(8,128)(4,1)S(1)}, pred[8,4,16]{2,0,1:T(8,128)(4,1)}, u32[]{:S(2)}) copy-start(pred[8,4,16]{2,0,1:T(8,128)(4,1)} %copy-done) | copy-start | bytes 1540
  78.2 8.5 %copy-start.2 = (f32[8,4,1]{0,1,2:T(4,128)S(1)}, f32[8,4,1]{0,1,2:T(4,128)}, u32[]{:S(2)}) copy-start(f32[8,4,1]{0,1,2:T(4,128)} %copy.64) | copy-start | bytes 388
  82.9 13.9 %all-to-all-start.1 = ((f32[8,4,1792]{2,1,0:T(4,128)}), f32[8,4,1792]{2,1,0:T(4,128)S(1)}, u32[]{:S(2)}, u32[]{:S(2)}) async-start(f32[8,4,1792]{2,1,0:T(4,128)} %fusion.8), calls=%async_computation.1 | async-start | bytes 458752 | tf_op jit(solution)/shard_map/all_to_all | solution.py:99
where the time goes:
time: 99.6 us; the launch traced here: 98.4 us
  local copies, waits for them, and re-layouts  32.3 us (32%)
  starting transfers between devices  30.9 us (31%)
  waiting for transfers between devices  18.1 us (18%)
  matrix products  11.8 us (12%)
  other arithmetic  5.09 us (5%)
    unnamed x22, local copies, waits for them, and re-layouts  18.8 us
    ppermute x3, starting transfers between devices, extended(): lax.ppermute(lax.slice_in_dim(block, block.shape[dim] - width, None, axis...  10.9 us
    all_to_all x1, waiting for transfers between devices, shards(): lax.all_to_all(bucket(coarse.reshape(elements, 7 * CDOF * CDOF)), 'gz', s...  9.83 us
    all_to_all x1, starting transfers between devices, shards(): lax.all_to_all(bucket(labels), 'gz', split_axis=0, concat_axis=0, tiled=T...  9.38 us
    dot_general x1, matrix products, shards(): jnp.einsum('xyzkij,xyzkjc->xyzkic', blocks, beside, precision=lax.Precisi...  7.55 us
    ppermute x3, starting transfers between devices, extended(): lax.ppermute(lax.slice_in_dim(block, 0, width, axis=dim), axis, backward)  6.85 us
    ppermute x3, waiting for transfers between devices, extended(): lax.ppermute(lax.slice_in_dim(block, 0, width, axis=dim), axis, backward)  4.8 us
    reshape x1, local copies, waits for them, and re-layouts, shards(): blocks = fine_blocks.reshape(size_x, size_y, size_z, 7, DOF, DOF)  4.35 us
  transfers between devices with their start and end apart: 8, of which 3 were waited for; matrix products, arithmetic and copies ran while one was open for 12% of the time, Pallas kernels for 0%

commit v1 on v0

v1 whole, which is shorter than its diff:
```python
import functools

import jax
import jax.numpy as jnp
from jax import lax
from jax.experimental import pallas as pl
from jax.experimental.pallas import tpu as pltpu
from jax.sharding import PartitionSpec as P

MESH = pl.DeviceIdType.MESH
F32 = jnp.float32
BF16 = jnp.bfloat16
AGGS = 8
FACES = 7
STEPS = ((0, 0, 0), (-1, 0, 0), (1, 0, 0), (0, -1, 0), (0, 1, 0), (0, 0, -1), (0, 0, 1))
ORDER = (4, 3, 5, 2, 6, 1, 7)
INNER = tuple((x, k) for x in range(2) for k in range(FACES) if (x, k) not in ((0, 1), (1, 2)))


def iota(shape, dim):
    return lax.broadcasted_iota(jnp.int32, shape, dim)


def split(value):
    high = value.astype(BF16)
    return high, (value - high.astype(F32)).astype(BF16)


def dot(a, b):
    return jnp.dot(a, b, preferred_element_type=F32)


def columns_of(slab):
    row, group = iota((64, 128), 0) & 7, iota((64, 128), 1) >> 4
    for bit in (4, 2, 1):
        row_bit, group_bit = row & bit, group & bit
        down = pltpu.roll(pltpu.roll(slab, 128 - 16 * bit, 1), bit, 0)
        up = pltpu.roll(pltpu.roll(slab, 16 * bit, 1), 64 - bit, 0)
        slab = jnp.where(row_bit == group_bit, slab, jnp.where(row_bit > 0, down, up))
    return slab


def stacked(cols):
    high, low = split(cols)
    return jnp.concatenate([high, low, high, low], axis=0)


def kernel(
    sizes, a_hbm, p_hbm, agg_hbm, own_hbm, out_ref,
    a_v, slabs, agg_v, own_v, acat, ycat, tcat, scat, msg, recv,
    local_sem, halo_send, halo_recv, send_sem, recv_sem, ready,
):
    nx, ny, nz = sizes
    gx, gy, gz = lax.axis_index("gx"), lax.axis_index("gy"), lax.axis_index("gz")

    def device(dx, dy, dz):
        return (
            lax.rem(gx + dx + nx, nx),
            lax.rem(gy + dy + ny, ny),
            lax.rem(gz + dz + nz, nz),
        )

    def signal(sem, target):
        pl.semaphore_signal(sem, inc=1, device_id=target, device_id_type=MESH)

    barrier = pltpu.get_barrier_semaphore()
    for step in STEPS[1:]:
        signal(barrier, device(*step))

    prolong_copies, fine_copies, index_copies = [], [], []
    for x in range(2):
        for y in range(2):
            c = x * 2 + y
            prolong_copies.append(
                pltpu.make_async_copy(
                    p_hbm.at[x, y], slabs.at[x, :, pl.ds(4 * y, 4), :], local_sem.at[c]
                )
            )
            rows = pl.ds(c * 896, 896)
            fine_copies.append(
                pltpu.make_async_copy(a_hbm.at[rows], a_v.at[rows], local_sem.at[4 + c])
            )
    for plane in range(4):
        where = jnp.clip(gx * 2 - 1 + plane, 0, 2 * nx - 1)
        index_copies.append(
            pltpu.make_async_copy(
                agg_hbm.at[pl.ds(where, 1)], agg_v.at[pl.ds(plane, 1)], local_sem.at[8 + plane]
            )
        )
    index_copies.append(pltpu.make_async_copy(own_hbm, own_v, local_sem.at[12]))
    for copy in prolong_copies + fine_copies + index_copies:
        copy.start()

    pl.semaphore_wait(barrier, 6)

    halo = []

    def halo_copy(src, dst, target):
        n = len(halo)
        halo.append(
            pltpu.make_async_remote_copy(
                src_ref=src, dst_ref=dst, send_sem=halo_send.at[n], recv_sem=halo_recv.at[n],
                device_id=target, device_id_type=MESH,
            )
        )
        halo[-1].start()

    for u in range(2):
        half = pl.ds(4 * u, 4)
        halo_copy(p_hbm.at[u, 1], slabs.at[4, :, half, :], device(0, 1, 0))
        halo_copy(p_hbm.at[u, 0], slabs.at[5, :, half, :], device(0, -1, 0))
        halo_copy(p_hbm.at[1, u], slabs.at[2, :, half, :], device(1, 0, 0))
        halo_copy(p_hbm.at[0, u], slabs.at[3, :, half, :], device(-1, 0, 0))
        for v in range(2):
            halo_copy(p_hbm.at[u, v, :, 3, :], slabs.at[6, :, u * 2 + v, :], device(0, 0, 1))
            halo_copy(p_hbm.at[u, v, :, 0, :], slabs.at[6, :, 4 + u * 2 + v, :], device(0, 0, -1))

    def greet(stage):
        for step in (-1, 1):
            signal(ready.at[stage], device(0, 0, step))

    greet(0)

    for copy in prolong_copies:
        copy.wait()
    own_cols = [columns_of(slabs[x].reshape(64, 128)) for x in range(2)]
    own_rhs = [stacked(cols) for cols in own_cols]
    turned = jnp.concatenate(split(jnp.concatenate(own_cols, axis=0).T), axis=0)
    lane = iota((128, 256), 1)
    spot = 2 * ((lane & 127) >> 2) + (lane >> 7)
    keep = ((iota((256, 256), 0) >> 4) & 3) == (iota((256, 256), 1) & 3)
    left = {}
    for x in range(2):
        spread = (iota((128, 256), 0) == spot + 64 * x).astype(BF16)
        wide = jnp.where(keep, dot(turned, spread), 0.0).astype(BF16)
        for y in range(2):
            parts = []
            for at in (y * 64, 128 + y * 64):
                rows = wide[at : at + 64]
                parts.append(jnp.concatenate([rows[:, :128], rows[:, 128:]], axis=0))
            left[x, y] = parts

    pl.semaphore_wait(ready.at[0], 2)
    greet(1)

    low_lanes = iota((64, 128), 1) < 64
    for x in range(2):
        for y in range(2):
            c = x * 2 + y
            fine_copies[c].wait()
            for k in range(FACES):
                high, low = split(a_v[pl.ds((c * FACES + k) * 128, 128), :])
                acat[c, 0:128, k * 128 : (k + 1) * 128] = high
                acat[c, 128:256, k * 128 : (k + 1) * 128] = low
            high, low = left[x, y]
            both = dot(jnp.concatenate([high, high], axis=1), acat[c]) + dot(low, acat[c, 0:128])
            for k in range(FACES):
                tile = both[:, k * 128 : (k + 1) * 128]
                tile = jnp.where(low_lanes, tile[0:64], tile[64:128])
                tile = tile + pltpu.roll(tile, 64, 1)
                high, low = split(tile)
                ycat[k, x, y * 64 : y * 64 + 64, 0:128] = high
                ycat[k, x, y * 64 : y * 64 + 64, 128:256] = low

    pl.semaphore_wait(ready.at[1], 2)
    greet(2)

    for copy in index_copies:
        copy.wait()
    agg_rows = agg_v[...].reshape(4 * 2 * ny, 4 * nz).astype(F32).astype(BF16)
    shape = (16, 4 * 2 * ny)
    line = iota(shape, 0)
    take = iota(shape, 1) == (line >> 2) * (2 * ny) + gy * 2 - 1 + (line & 3)
    near = dot(take.astype(BF16), agg_rows).astype(BF16)
    shape = (4 * nz, 384)
    lane = iota(shape, 1)
    take = iota(shape, 0) == gz * 4 + ((lane >> 3) & 3) + (lane >> 7) - 1
    near = dot(near, take.astype(BF16))
    lane = iota((1, 128), 1)
    element, z_at, y_high = (lane >> 3) & 7, (lane >> 3) & 3, ((lane >> 5) & 1) == 1

    def slot(x, dx, dy, dz):
        lanes = slice((dz + 1) * 128, (dz + 2) * 128)
        row = (x + 1 + dx) * 4 + 1 + dy
        return jnp.where(y_high, near[row + 1 : row + 2, lanes], near[row : row + 1, lanes])

    slots = [[slot(x, *step) for step in STEPS] for x in range(2)]
    owners = own_v[0].astype(F32)
    owner = [jnp.zeros((1, 128), F32)] * 2
    for s in range(AGGS):
        value = jnp.broadcast_to(owners[:, s : s + 1], (1, 128))
        owner = [jnp.where(slots[x][0] == s, value, owner[x]) for x in range(2)]
    place = [jnp.zeros((1, 128), F32)] * 2
    for m in range(AGGS):
        turn = [pltpu.roll(owner[x], 8 * m, 1) if m else owner[x] for x in range(2)]
        if m:
            for x in range(2):
                place[x] += jnp.where((turn[x] == owner[x]) & (element >= m), 1.0, 0.0)
        place[1] += jnp.where(turn[0] == owner[1], 1.0, 0.0)
    code = [owner[x] * 8.0 + place[x] for x in range(2)]

    row64 = iota((64, 128), 0).astype(F32)

    def selection(codes):
        return (row64 == codes).astype(BF16)

    for n, (x, k) in enumerate(INNER):
        codes = owner[x] * 8.0 + slots[x][k]
        valid = {3: y_high, 4: ~y_high, 5: z_at >= 1, 6: z_at <= 2}.get(k)
        if valid is not None:
            codes = jnp.where(valid, codes, -1.0)
        scat[:, n * 128 : (n + 1) * 128] = selection(codes)

    fold = ((iota((256, 128), 0) & 15) == (iota((256, 128), 1) & 15)).astype(BF16)
    row_e, lane_e = iota((128, 128), 0) >> 4, iota((128, 128), 1) >> 4
    on_c = (iota((128, 128), 0) & 7) == lane_e

    def terms(lhs, rhs, shift):
        block = jnp.where(row_e + shift == lane_e, dot(lhs, rhs), 0.0)
        tall = jnp.where(on_c, dot(jnp.concatenate(split(block), axis=1), fold), 0.0)
        tall = tall.reshape(8, 16, 128)
        tall = jnp.concatenate(
            [tall[:, 0:8].reshape(64, 128), tall[:, 8:16].reshape(64, 128)], axis=1
        )
        return jnp.concatenate(split(tall), axis=0)

    shifts = {3: -4, 4: 4, 5: -1, 6: 1}
    for n, (x, k) in enumerate(INNER):
        other = {1: 0, 2: 1}.get(k, x)
        tcat[n * 128 : (n + 1) * 128, :] = terms(ycat[k, x], own_rhs[other], shifts.get(k, 0))

    copies = []

    def send(stage, rows):
        for o in range(AGGS):
            for h in range(2):
                msg[pl.ds(o * 48 + stage * 16 + h * 8, 8), :] = rows[
                    o * 8 : o * 8 + 8, h * 128 : (h + 1) * 128
                ]
        target_rows = pl.ds(pl.multiple_of(gz * 48 + stage * 16, 16), 16)
        for d in ORDER:
            target = device(0, 0, d)
            copy = pltpu.make_async_remote_copy(
                src_ref=msg.at[pl.ds(pl.multiple_of(target[2] * 48 + stage * 16, 16), 16)],
                dst_ref=recv.at[target_rows],
                send_sem=send_sem.at[stage, d], recv_sem=recv_sem.at[stage, d],
                device_id=target, device_id_type=MESH,
            )
            copy.start()
            copies.append(copy)
        copy = pltpu.make_async_copy(
            msg.at[target_rows], recv.at[target_rows], recv_sem.at[stage, 0]
        )
        copy.start()
        copies.append(copy)

    pl.semaphore_wait(ready.at[2], 2)
    send(0, dot(scat[...], tcat[...]))

    inside = (gx > 0, gx < nx - 1, gy > 0, gy < ny - 1, gz > 0, gz < nz - 1)

    def when(flag, value, other):
        return jnp.where(jnp.full((1, 128), flag), value, other)

    label = [
        [
            when(inside[0], slots[0][1] + 1.0, 0.0),
            when(inside[1], slots[1][2] + 9.0, 0.0),
        ],
        [
            jnp.where(
                y_high,
                when(inside[3], slots[x][4] + 9.0, 0.0),
                when(inside[2], slots[x][3] + 1.0, 0.0),
            )
            for x in range(2)
        ],
        [
            jnp.where(
                z_at == 0,
                when(inside[4], slots[x][5] + 1.0, 0.0),
                jnp.where(z_at == 3, when(inside[5], slots[x][6] + 9.0, 0.0), 0.0),
            )
            for x in range(2)
        ],
    ]
    row, lane_all = iota((128, 128), 0), iota((128, 128), 1)
    once = ((lane_all & 7) == 0) & (lane_all < 64)
    which, who = [], []
    for x in range(2):
        value = jnp.where(
            row < 4, label[0][x], jnp.where(row < 8, label[1][x], jnp.where(row < 12, label[2][x], 0.0))
        )
        value = jnp.where(once & ((row & 3).astype(F32) == place[x]), value, 0.0)
        which.append(value.astype(BF16))
        row_o = iota((64, 128), 0)
        who.append((((row_o & 7) == 4) & ((row_o >> 3).astype(F32) == owner[x])).astype(BF16))
    labels = lax.dot_general(
        jnp.concatenate(who, axis=1), jnp.concatenate(which, axis=1),
        (((1,), (1,)), ((), ())), preferred_element_type=F32,
    )

    edge_codes = [
        code[0],
        code[1],
        jnp.where(y_high, pltpu.roll(code[1], 32, 1), code[0]) + 4.0,
        jnp.where(y_high, code[1], pltpu.roll(code[0], 96, 1)) + 4.0,
    ]
    edge_codes = [when(inside[i], edge_codes[i], -1.0) for i in range(4)]
    z_code = jnp.full((1, 128), -1.0, F32)
    for side in range(2):
        for x in range(2):
            for y in range(2):
                to, at = side * 4 + x * 2 + y, y * 4 + side * 3
                turn = (8 * (to - at)) % 128
                value = pltpu.roll(code[x], turn, 1) if turn else code[x]
                z_code = jnp.where(element == to, when(inside[4 + side], value, -1.0), z_code)

    for copy in halo:
        copy.wait()

    def halo_rhs(i):
        return stacked(columns_of(slabs[i].reshape(64, 128)))

    def rows_y(k, y):
        return jnp.concatenate([ycat[k, x, y * 64 : y * 64 + 64] for x in range(2)], axis=0)

    def rows_z(k, z):
        return [
            ycat[k, x, y * 64 + z * 16 : y * 64 + z * 16 + 16] for x in range(2) for y in range(2)
        ]

    edges = jnp.concatenate(
        [
            terms(ycat[1, 0], halo_rhs(2), 0),
            terms(ycat[2, 1], halo_rhs(3), 0),
            terms(rows_y(3, 0), halo_rhs(4), 0),
            terms(rows_y(4, 1), halo_rhs(5), 0),
        ],
        axis=0,
    )
    send(1, dot(jnp.concatenate([selection(c) for c in edge_codes], axis=1), edges))
    edges = terms(jnp.concatenate(rows_z(5, 0) + rows_z(6, 3), axis=0), halo_rhs(6), 0)
    edges = dot(selection(z_code), edges)
    send(2, jnp.concatenate([edges[:, :128] + labels, edges[:, 128:]], axis=1))

    per_stage = len(ORDER) + 1

    def arrive(stage):
        for copy in copies[stage * per_stage : stage * per_stage + per_stage - 1]:
            copy.wait()
        copies[stage * per_stage + per_stage - 1].wait()

    def came(stage, h, r):
        return recv[pl.ds(stage * 16 + h * 8 + r, 8, stride=48), :]

    arrive(0)
    for s in range(AGGS):
        for h in range(2):
            out_ref[:, s * 256 + h * 128 : s * 256 + h * 128 + 128] = came(0, h, s)
    arrive(1)
    arrive(2)
    marks = came(2, 0, 4)
    for axis in range(3):
        stage, at = (1, axis * 4) if axis < 2 else (2, 0)
        values = [[came(stage, h, at + p) for h in range(2)] for p in range(4)]
        tags = [
            jnp.broadcast_to(marks[:, axis * 4 + p : axis * 4 + p + 1], (8, 128)) for p in range(4)
        ]
        for column in range(16):
            hits = [tag == column + 1.0 for tag in tags]
            for h in range(2):
                total = jnp.where(hits[0], values[0][h], 0.0)
                for p in range(1, 4):
                    total += jnp.where(hits[p], values[p][h], 0.0)
                at_lane = (AGGS * (1 + 2 * axis) + column) * 256 + h * 128
                out_ref[:, at_lane : at_lane + 128] = total


def solution(mesh):
    sizes = (mesh.shape["gx"], mesh.shape["gy"], mesh.shape["gz"])

    def shards(fine_blocks, prolong, agg_map, owner_map):
        fine = fine_blocks.transpose(0, 1, 3, 2, 4).reshape(2, 2, 7, 4, 32, 128)
        fine = fine.transpose(0, 1, 2, 4, 3, 5).reshape(3584, 128)
        base = prolong.reshape(2, 2, 4, 8, 128).transpose(0, 1, 3, 2, 4)
        inner = len(INNER) * 128
        result = pl.pallas_call(
            functools.partial(kernel, sizes),
            out_shape=jax.ShapeDtypeStruct((AGGS, 7 * AGGS * 256), F32),
            in_specs=[pl.BlockSpec(memory_space=pl.ANY)] * 4,
            out_specs=pl.BlockSpec(memory_space=pltpu.VMEM),
            scratch_shapes=[
                pltpu.VMEM((3584, 128), F32),
                pltpu.VMEM((7, 8, 8, 128), F32),
                pltpu.VMEM((4,) + agg_map.shape[1:], jnp.int32),
                pltpu.VMEM((1, 1, AGGS), jnp.int32),
                pltpu.VMEM((4, 256, 896), BF16),
                pltpu.VMEM((7, 2, 128, 256), BF16),
                pltpu.VMEM((inner, 256), BF16),
                pltpu.VMEM((64, inner), BF16),
                pltpu.VMEM((384, 128), F32),
                pltpu.VMEM((384, 128), F32),
                pltpu.SemaphoreType.DMA((13,)),
                pltpu.SemaphoreType.DMA((16,)),
                pltpu.SemaphoreType.DMA((16,)),
                pltpu.SemaphoreType.DMA((3, 8)),
                pltpu.SemaphoreType.DMA((3, 8)),
                pltpu.SemaphoreType.REGULAR((3,)),
            ],
            compiler_params=pltpu.CompilerParams(collective_id=0, has_side_effects=True),
        )(fine, base, agg_map, owner_map)
        return result.reshape(1, 1, AGGS, 7 * AGGS * 256)

    placed = (P("gx", "gy", "gz", None, None), P("gx", "gy", "gz", None), P(), P("gx", "gy", "gz"))
    return jax.shard_map(
        shards, mesh=mesh, in_specs=placed, out_specs=P("gx", "gy", "gz", None), check_vma=False
    )
```

time: 99.6 us -> 32.2 us (0.32)
  the two profiles are of different devices: /device:TPU:194 before, /device:TPU:6 now
where the time goes in v1:
time: 32.2 us; the launch traced here: 32 us
  Pallas kernels  30.2 us (94%)
  local copies, waits for them, and re-layouts  1.82 us (6%)
    pallas_call x1, Pallas kernels, shards(): pl.pallas_call(functools.partial(kernel, sizes), out_shape=jax.ShapeDtype...  30.2 us
    unnamed x1, local copies, waits for them, and re-layouts  1.82 us

profile of v1, /device:TPU:6, one launch (start us, length us, event | category | flops | bytes accessed | tf_op | source)
XLA Modules:
  0.0 32.0 jit_solution(6935205582328237004)
XLA Ops:
  0.0 30.2 %shard_map.46 = f32[8,14336]{1,0:T(8,128)} custom-call(f32[3584,128]{1,0:T(8,128)} %bitcast.11, f32[2,2,8,4,128]{4,3,2,1,0:T(4,128)} %bitcast.13, s32[16,24,32]{2,1,0:T(8,128)} %agg_hbm.1, s32[1,1,8]{2,1,0:T(1,128)} %own_hbm.1), custom_call_target="tpu_custom_call" | custom-call | tf_op jit(solution)/shard_map/pallas_call | solution.py:388
  30.2 1.8 %copy.7 = f32[1,1,8,14336]{3,2,1,0:T(8,128)} copy(f32[1,1,8,14336]{3,2,1,0:T(8,128)} %bitcast.12) | data formatting | bytes 917504

commit v2 on v1

--- a/solution.py
+++ b/solution.py
@@ -10,6 +10,7 @@
 MESH = pl.DeviceIdType.MESH
 F32 = jnp.float32
 BF16 = jnp.bfloat16
+MEET_AT = 0
 AGGS = 8
 FACES = 7
 STEPS = ((0, 0, 0), (-1, 0, 0), (1, 0, 0), (0, -1, 0), (0, 1, 0), (0, 0, -1), (0, 0, 1))
@@ -46,8 +47,8 @@
 
 
 def kernel(
-    sizes, a_hbm, p_hbm, agg_hbm, own_hbm, out_ref,
-    a_v, slabs, agg_v, own_v, acat, ycat, tcat, scat, msg, recv,
+    sizes, a_hbm, p_hbm, agg_hbm, own_hbm, recv,
+    a_v, slabs, agg_v, own_v, acat, ycat, tcat, scat, msg,
     local_sem, halo_send, halo_recv, send_sem, recv_sem, ready,
 ):
     nx, ny, nz = sizes
@@ -63,9 +64,14 @@
     def signal(sem, target):
         pl.semaphore_signal(sem, inc=1, device_id=target, device_id_type=MESH)
 
+    inside = (gx > 0, gx < nx - 1, gy > 0, gy < ny - 1, gz > 0, gz < nz - 1)
+
     barrier = pltpu.get_barrier_semaphore()
-    for step in STEPS[1:]:
-        signal(barrier, device(*step))
+    for n, step in enumerate(STEPS[1:]):
+        if n < 4:
+            pl.when(inside[n])(functools.partial(signal, barrier, device(*step)))
+        else:
+            signal(barrier, device(*step))
 
     prolong_copies, fine_copies, index_copies = [], [], []
     for x in range(2):
@@ -91,35 +97,54 @@
     for copy in prolong_copies + fine_copies + index_copies:
         copy.start()
 
-    pl.semaphore_wait(barrier, 6)
-
-    halo = []
-
-    def halo_copy(src, dst, target):
-        n = len(halo)
-        halo.append(
+    halo = [[] for _ in range(6)]
+    used = [0]
+
+    def halo_copy(face, src, dst):
+        n = used[0]
+        used[0] += 1
+        halo[face].append(
             pltpu.make_async_remote_copy(
                 src_ref=src, dst_ref=dst, send_sem=halo_send.at[n], recv_sem=halo_recv.at[n],
-                device_id=target, device_id_type=MESH,
-            )
-        )
-        halo[-1].start()
+                device_id=device(*STEPS[1 + face]), device_id_type=MESH,
+            )
+        )
 
     for u in range(2):
         half = pl.ds(4 * u, 4)
-        halo_copy(p_hbm.at[u, 1], slabs.at[4, :, half, :], device(0, 1, 0))
-        halo_copy(p_hbm.at[u, 0], slabs.at[5, :, half, :], device(0, -1, 0))
-        halo_copy(p_hbm.at[1, u], slabs.at[2, :, half, :], device(1, 0, 0))
-        halo_copy(p_hbm.at[0, u], slabs.at[3, :, half, :], device(-1, 0, 0))
+        halo_copy(0, p_hbm.at[0, u], slabs.at[3, :, half, :])
+        halo_copy(1, p_hbm.at[1, u], slabs.at[2, :, half, :])
+        halo_copy(2, p_hbm.at[u, 0], slabs.at[5, :, half, :])
+        halo_copy(3, p_hbm.at[u, 1], slabs.at[4, :, half, :])
         for v in range(2):
-            halo_copy(p_hbm.at[u, v, :, 3, :], slabs.at[6, :, u * 2 + v, :], device(0, 0, 1))
-            halo_copy(p_hbm.at[u, v, :, 0, :], slabs.at[6, :, 4 + u * 2 + v, :], device(0, 0, -1))
+            halo_copy(4, p_hbm.at[u, v, :, 0, :], slabs.at[6, :, 4 + u * 2 + v, :])
+            halo_copy(5, p_hbm.at[u, v, :, 3, :], slabs.at[6, :, u * 2 + v, :])
 
     def greet(stage):
         for step in (-1, 1):
             signal(ready.at[stage], device(0, 0, step))
 
-    greet(0)
+    def meet():
+        pl.semaphore_wait(barrier, 2 + sum(flag.astype(jnp.int32) for flag in inside[:4]))
+        for face in (2, 3, 4, 5, 0, 1):
+
+            @pl.when(inside[face])
+            def _():
+                for copy in halo[face]:
+                    copy.start()
+
+        greet(0)
+        for face in range(4):
+
+            @pl.when(~inside[face])
+            def _():
+                slabs[2 + face] = jnp.zeros((8, 8, 128), F32)
+
+        for face in (4, 5):
+
+            @pl.when(~inside[face])
+            def _():
+                slabs[6, :, (face - 4) * 4 : (face - 4) * 4 + 4, :] = jnp.zeros((8, 4, 128), F32)
 
     for copy in prolong_copies:
         copy.wait()
@@ -140,9 +165,6 @@
                 parts.append(jnp.concatenate([rows[:, :128], rows[:, 128:]], axis=0))
             left[x, y] = parts
 
-    pl.semaphore_wait(ready.at[0], 2)
-    greet(1)
-
     low_lanes = iota((64, 128), 1) < 64
     for x in range(2):
         for y in range(2):
@@ -161,9 +183,14 @@
                 high, low = split(tile)
                 ycat[k, x, y * 64 : y * 64 + 64, 0:128] = high
                 ycat[k, x, y * 64 : y * 64 + 64, 128:256] = low
-
-    pl.semaphore_wait(ready.at[1], 2)
-    greet(2)
+            if c == MEET_AT:
+                meet()
+            if c == 2:
+                pl.semaphore_wait(ready.at[0], 2)
+                greet(1)
+            if c == 3:
+                pl.semaphore_wait(ready.at[1], 2)
+                greet(2)
 
     for copy in index_copies:
         copy.wait()
@@ -256,8 +283,6 @@
 
     pl.semaphore_wait(ready.at[2], 2)
     send(0, dot(scat[...], tcat[...]))
-
-    inside = (gx > 0, gx < nx - 1, gy > 0, gy < ny - 1, gz > 0, gz < nz - 1)
 
     def when(flag, value, other):
         return jnp.where(jnp.full((1, 128), flag), value, other)
@@ -316,8 +341,13 @@
                 value = pltpu.roll(code[x], turn, 1) if turn else code[x]
                 z_code = jnp.where(element == to, when(inside[4 + side], value, -1.0), z_code)
 
-    for copy in halo:
-        copy.wait()
+    for face in range(6):
+
+        @pl.when(inside[face])
+        def _():
+            for mine, theirs in zip(halo[face], halo[face ^ 1]):
+                mine.wait_send()
+                theirs.wait_recv()
 
     def halo_rhs(i):
         return stacked(columns_of(slabs[i].reshape(64, 128)))
@@ -344,22 +374,17 @@
     edges = dot(selection(z_code), edges)
     send(2, jnp.concatenate([edges[:, :128] + labels, edges[:, 128:]], axis=1))
 
-    per_stage = len(ORDER) + 1
-
-    def arrive(stage):
-        for copy in copies[stage * per_stage : stage * per_stage + per_stage - 1]:
-            copy.wait()
-        copies[stage * per_stage + per_stage - 1].wait()
-
+    for copy in copies:
+        copy.wait()
+
+
+def spread(recv, out_ref):
     def came(stage, h, r):
         return recv[pl.ds(stage * 16 + h * 8 + r, 8, stride=48), :]
 
-    arrive(0)
     for s in range(AGGS):
         for h in range(2):
             out_ref[:, s * 256 + h * 128 : s * 256 + h * 128 + 128] = came(0, h, s)
-    arrive(1)
-    arrive(2)
     marks = came(2, 0, 4)
     for axis in range(3):
         stage, at = (1, axis * 4) if axis < 2 else (2, 0)
@@ -385,9 +410,9 @@
         fine = fine.transpose(0, 1, 2, 4, 3, 5).reshape(3584, 128)
         base = prolong.reshape(2, 2, 4, 8, 128).transpose(0, 1, 3, 2, 4)
         inner = len(INNER) * 128
-        result = pl.pallas_call(
+        rows = pl.pallas_call(
             functools.partial(kernel, sizes),
-            out_shape=jax.ShapeDtypeStruct((AGGS, 7 * AGGS * 256), F32),
+            out_shape=jax.ShapeDtypeStruct((384, 128), F32),
             in_specs=[pl.BlockSpec(memory_space=pl.ANY)] * 4,
             out_specs=pl.BlockSpec(memory_space=pltpu.VMEM),
             scratch_shapes=[
@@ -400,7 +425,6 @@
                 pltpu.VMEM((inner, 256), BF16),
                 pltpu.VMEM((64, inner), BF16),
                 pltpu.VMEM((384, 128), F32),
-                pltpu.VMEM((384, 128), F32),
                 pltpu.SemaphoreType.DMA((13,)),
                 pltpu.SemaphoreType.DMA((16,)),
                 pltpu.SemaphoreType.DMA((16,)),
@@ -410,6 +434,12 @@
             ],
             compiler_params=pltpu.CompilerParams(collective_id=0, has_side_effects=True),
         )(fine, base, agg_map, owner_map)
+        result = pl.pallas_call(
+            spread,
+            out_shape=jax.ShapeDtypeStruct((AGGS, 7 * AGGS * 256), F32),
+            in_specs=[pl.BlockSpec(memory_space=pltpu.VMEM)],
+            out_specs=pl.BlockSpec(memory_space=pltpu.VMEM),
+        )(rows)
         return result.reshape(1, 1, AGGS, 7 * AGGS * 256)
 
     placed = (P("gx", "gy", "gz", None, None), P("gx", "gy", "gz", None), P(), P("gx", "gy", "gz"))

time: 32.2 us -> 25.8 us (0.80)
  the two profiles are of different devices: /device:TPU:6 before, /device:TPU:8 now
where the time goes in v2:
time: 25.8 us; the launch traced here: 25.6 us
  Pallas kernels  25.6 us (99%)
    pallas_call x1, Pallas kernels, shards(): pl.pallas_call(functools.partial(kernel, sizes), out_shape=jax.ShapeDtype...  23.7 us
    pallas_call x1, Pallas kernels, shards(): pl.pallas_call(spread, out_shape=jax.ShapeDtypeStruct((AGGS, 7 * AGGS * 2...  1.9 us

profile of v2, /device:TPU:8, one launch (start us, length us, event | category | flops | bytes accessed | tf_op | source)
XLA Modules:
  0.0 25.6 jit_solution(9573817375428998442)
XLA Ops:
  0.0 23.7 %shard_map.46.recv = f32[384,128]{1,0:T(8,128)} custom-call(f32[3584,128]{1,0:T(8,128)} %bitcast.11, f32[2,2,8,4,128]{4,3,2,1,0:T(4,128)} %bitcast.12, s32[16,24,32]{2,1,0:T(8,128)} %agg_hbm.1, s32[1,1,8]{2,1,0:T(1,128)} %own_hbm.1), custom_call_target="tpu_custom_call" | custom-call | tf_op jit(solution)/shard_map/pallas_call | solution.py:413
  23.7 1.9 %shard_map.47 = f32[8,14336]{1,0:T(8,128)} custom-call(f32[384,128]{1,0:T(8,128)} %shard_map.46.recv), custom_call_target="tpu_custom_call" | custom-call | tf_op jit(solution)/shard_map/pallas_call | solution.py:437

commit v3 on v2

v3 whole, which is shorter than its diff:
```python
import functools

import jax
import jax.numpy as jnp
from jax import lax
from jax.experimental import pallas as pl
from jax.experimental.pallas import tpu as pltpu
from jax.sharding import PartitionSpec as P

MESH = pl.DeviceIdType.MESH
F32 = jnp.float32
BF16 = jnp.bfloat16
AGGS = 8
FACES = 7
STEPS = ((0, 0, 0), (-1, 0, 0), (1, 0, 0), (0, -1, 0), (0, 1, 0), (0, 0, -1), (0, 0, 1))


def iota(shape, dim):
    return lax.broadcasted_iota(jnp.int32, shape, dim)


def split(value):
    high = value.astype(BF16)
    return high, (value - high.astype(F32)).astype(BF16)


def dot(a, b):
    return jnp.dot(a, b, preferred_element_type=F32)


def columns_of(slab):
    row, group = iota((8, 8, 128), 1), iota((8, 8, 128), 2) >> 4
    for bit in (4, 2, 1):
        row_bit, group_bit = row & bit, group & bit
        down = pltpu.roll(pltpu.roll(slab, 128 - 16 * bit, 2), bit, 1)
        if bit == 4:
            slab = jnp.where(row_bit == group_bit, slab, down)
        else:
            up = pltpu.roll(pltpu.roll(slab, 16 * bit, 2), 8 - bit, 1)
            slab = jnp.where(row_bit == group_bit, slab, jnp.where(row_bit > 0, down, up))
    return slab.reshape(64, 128)


def stacked(cols):
    high, low = split(cols)
    return jnp.concatenate([high, low, high, low], axis=0)


def kernel(
    sizes, a_hbm, p_hbm, agg_hbm, own_hbm, recv,
    a_v, slabs, agg_v, own_v, yv, msg,
    local_sem, halo_send, halo_recv, row_send, row_recv, ready,
):
    nx, ny, nz = sizes
    gx, gy, gz = lax.axis_index("gx"), lax.axis_index("gy"), lax.axis_index("gz")

    def device(dx, dy, dz):
        return (
            lax.rem(gx + dx + nx, nx),
            lax.rem(gy + dy + ny, ny),
            lax.rem(gz + dz + nz, nz),
        )

    def signal(sem, target):
        pl.semaphore_signal(sem, inc=1, device_id=target, device_id_type=MESH)

    inside = (gx > 0, gx < nx - 1, gy > 0, gy < ny - 1, gz > 0, gz < nz - 1)

    barrier = pltpu.get_barrier_semaphore()
    for n, step in enumerate(STEPS[1:]):
        if n < 4:
            pl.when(inside[n])(functools.partial(signal, barrier, device(*step)))
        else:
            signal(barrier, device(*step))

    def copied(dst, n):
        return pltpu.make_async_copy(dst, dst, local_sem.at[n])

    for x in range(2):
        for y in range(2):
            half = pl.ds(4 * y, 4)
            pltpu.make_async_copy(
                p_hbm.at[x, y], slabs.at[x, :, half, :], local_sem.at[0]
            ).start()
    for c in range(4):
        rows = pl.ds(c * 896, 896)
        pltpu.make_async_copy(a_hbm.at[rows], a_v.at[rows], local_sem.at[1]).start()
    for plane in range(4):
        where = jnp.clip(gx * 2 - 1 + plane, 0, 2 * nx - 1)
        pltpu.make_async_copy(
            agg_hbm.at[pl.ds(where, 1)], agg_v.at[pl.ds(plane, 1)], local_sem.at[2]
        ).start()
    pltpu.make_async_copy(own_hbm, own_v, local_sem.at[3]).start()

    halo = [[] for _ in range(6)]

    def halo_copy(face, src, dst):
        halo[face].append(
            pltpu.make_async_remote_copy(
                src_ref=src, dst_ref=dst,
                send_sem=halo_send.at[face], recv_sem=halo_recv.at[face],
                device_id=device(*STEPS[1 + face]), device_id_type=MESH,
            )
        )

    for u in range(2):
        half = pl.ds(4 * u, 4)
        halo_copy(0, p_hbm.at[0, u], slabs.at[3, :, half, :])
        halo_copy(1, p_hbm.at[1, u], slabs.at[2, :, half, :])
        halo_copy(2, p_hbm.at[u, 0], slabs.at[5, :, half, :])
        halo_copy(3, p_hbm.at[u, 1], slabs.at[4, :, half, :])
        for v in range(2):
            halo_copy(4, p_hbm.at[u, v, :, 0, :], slabs.at[6, :, 4 + u * 2 + v, :])
            halo_copy(5, p_hbm.at[u, v, :, 3, :], slabs.at[6, :, u * 2 + v, :])

    def halo_wait(face):
        slab = slabs.at[2 + face] if face < 4 else slabs.at[6, :, pl.ds((face - 4) * 4, 4), :]
        done = pltpu.make_async_remote_copy(
            src_ref=slab, dst_ref=slab,
            send_sem=halo_send.at[face], recv_sem=halo_recv.at[face ^ 1],
            device_id=device(*STEPS[1 + face]), device_id_type=MESH,
        )
        done.wait_send()
        done.wait_recv()

    def tell(stage):
        for step in (-1, 1):
            signal(ready.at[stage], device(0, 0, step))

    def learn(stage):
        pl.semaphore_wait(ready.at[stage], 2)
        if stage < 2:
            tell(stage + 1)

    def meet():
        pl.semaphore_wait(barrier, 2 + sum(flag.astype(jnp.int32) for flag in inside[:4]))
        for face in (2, 3, 4, 5, 0, 1):

            @pl.when(inside[face])
            def _():
                for copy in halo[face]:
                    copy.start()

        tell(0)
        for face in range(4):

            @pl.when(~inside[face])
            def _():
                slabs[2 + face] = jnp.zeros((8, 8, 128), F32)

        for face in (4, 5):

            @pl.when(~inside[face])
            def _():
                slabs[6, :, (face - 4) * 4 : (face - 4) * 4 + 4, :] = jnp.zeros((8, 4, 128), F32)

    copied(slabs.at[pl.ds(0, 2)], 0).wait()
    own_cols = [columns_of(slabs[x]) for x in range(2)]
    own_rhs = [stacked(cols) for cols in own_cols]
    turned = jnp.concatenate(split(jnp.concatenate(own_cols, axis=0).T), axis=0)
    lane = iota((128, 256), 1)
    spot = 2 * ((lane & 127) >> 2) + (lane >> 7)
    keep = ((iota((256, 256), 0) >> 4) & 3) == (iota((256, 256), 1) & 3)
    left = {}
    for x in range(2):
        spread = (iota((128, 256), 0) == spot + 64 * x).astype(BF16)
        wide = jnp.where(keep, dot(turned, spread), 0.0).astype(BF16)
        for y in range(2):
            parts = []
            for at in (y * 64, 128 + y * 64):
                rows = wide[at : at + 64]
                parts.append(jnp.concatenate([rows[:, :128], rows[:, 128:]], axis=0))
            left[x, y] = parts

    meet()

    low_lanes = iota((64, 128), 1) < 64
    copied(a_v, 1).wait()
    for x in range(2):
        for y in range(2):
            c = x * 2 + y
            blocks = [split(a_v[pl.ds((c * FACES + k) * 128, 128), :]) for k in range(FACES)]
            highs = jnp.concatenate([block[0] for block in blocks], axis=1)
            lows = jnp.concatenate([block[1] for block in blocks], axis=1)
            high, low = left[x, y]
            stack = jnp.concatenate([high, low], axis=0)
            both = dot(
                jnp.concatenate([stack, stack], axis=1), jnp.concatenate([highs, lows], axis=0)
            )
            for k in range(FACES):
                tile = both[:, k * 128 : (k + 1) * 128]
                tile = jnp.where(low_lanes, tile[0:64] + tile[128:192], tile[64:128] + tile[192:256])
                yv[k, x, y * 64 : y * 64 + 64, :] = tile + pltpu.roll(tile, 64, 1)
    learn(0)

    copied(agg_v, 2).wait()
    copied(own_v, 3).wait()
    agg_rows = agg_v[...].reshape(4 * 2 * ny, 4 * nz).astype(F32).astype(BF16)
    shape = (16, 4 * 2 * ny)
    line = iota(shape, 0)
    take = iota(shape, 1) == (line >> 2) * (2 * ny) + gy * 2 - 1 + (line & 3)
    near = dot(take.astype(BF16), agg_rows).astype(BF16)
    shape = (4 * nz, 384)
    lane = iota(shape, 1)
    take = iota(shape, 0) == gz * 4 + ((lane >> 3) & 3) + (lane >> 7) - 1
    near = dot(near, take.astype(BF16))
    lane = iota((1, 128), 1)
    element, z_at, y_high = (lane >> 3) & 7, (lane >> 3) & 3, ((lane >> 5) & 1) == 1

    def slot(x, dx, dy, dz):
        lanes = slice((dz + 1) * 128, (dz + 2) * 128)
        row = (x + 1 + dx) * 4 + 1 + dy
        return jnp.where(y_high, near[row + 1 : row + 2, lanes], near[row : row + 1, lanes])

    slots = [[slot(x, *step) for step in STEPS] for x in range(2)]
    owners = own_v[0].astype(F32)
    owner = [jnp.zeros((1, 128), F32)] * 2
    for s in range(AGGS):
        value = jnp.broadcast_to(owners[:, s : s + 1], (1, 128))
        owner = [jnp.where(slots[x][0] == s, value, owner[x]) for x in range(2)]
    place = [jnp.zeros((1, 128), F32)] * 2
    for m in range(AGGS):
        turn = [pltpu.roll(owner[x], 8 * m, 1) if m else owner[x] for x in range(2)]
        if m:
            for x in range(2):
                place[x] += jnp.where((turn[x] == owner[x]) & (element >= m), 1.0, 0.0)
        place[1] += jnp.where(turn[0] == owner[1], 1.0, 0.0)
    code = [owner[x] * 8.0 + place[x] for x in range(2)]

    row64 = iota((64, 128), 0).astype(F32)

    def selection(codes):
        return (row64 == codes).astype(BF16)

    fold = ((iota((256, 128), 0) & 15) == (iota((256, 128), 1) & 15)).astype(BF16)
    group = iota((16, 128), 1) >> 4

    def terms(lhs, rhs, partners, places=tuple(range(8))):
        count = len(partners)
        block = dot(jnp.concatenate(split(lhs), axis=1), rhs)
        block = jnp.concatenate(
            [
                jnp.where(group == partner, block[i * 16 : i * 16 + 16], 0.0)
                for i, partner in enumerate(partners)
            ],
            axis=0,
        )
        tall = dot(jnp.concatenate(split(block), axis=1), fold).reshape(count * 2, 8, 128)
        on_c = iota((count * 2, 8, 128), 1) == (iota((count * 2, 8, 128), 2) >> 4)
        tall = jnp.where(on_c, tall, 0.0).reshape(count, 2, 8, 128)
        rows = [jnp.zeros((8, 256), F32)] * 8
        for i, at in enumerate(places):
            rows[at] = jnp.concatenate([tall[i, 0], tall[i, 1]], axis=1)
        return jnp.concatenate(split(jnp.concatenate(rows, axis=0)), axis=0)

    own = tuple(range(8))
    z_odd = (z_at & 1) == 1
    inner_rows = jnp.zeros((64, 256), F32)
    for x in range(2):
        y = [yv[k, x] for k in range(FACES)]
        at = [[y[k][e * 16 : e * 16 + 16] for e in range(8)] for k in (5, 6)]
        cross = 2 - x
        tiles = [
            (y[0], own_rhs[x], own, own, slots[x][0]),
            (y[cross], own_rhs[1 - x], own, own, slots[x][cross]),
            (
                jnp.concatenate([y[4][:64], y[3][64:]], axis=0), own_rhs[x],
                tuple(e ^ 4 for e in own), own, jnp.where(y_high, slots[x][3], slots[x][4]),
            ),
            (
                jnp.concatenate([at[1 - (e & 1)][e] for e in own], axis=0), own_rhs[x],
                tuple(e ^ 1 for e in own), own, jnp.where(z_odd, slots[x][5], slots[x][6]),
            ),
            (
                jnp.concatenate([at[e & 1][e] for e in (1, 2, 5, 6)], axis=0), own_rhs[x],
                (2, 1, 6, 5), (1, 2, 5, 6),
                jnp.where(
                    z_at == 1, slots[x][6], jnp.where(z_at == 2, slots[x][5], -1000.0)
                ),
            ),
        ]
        for lhs, rhs, partners, places, column in tiles:
            inner_rows += dot(selection(owner[x] * 8.0 + column), terms(lhs, rhs, partners, places))

    def put(at, rows):
        for o in range(AGGS):
            for h in range(2):
                msg[pl.ds(o * 48 + at + h * 8, 8), :] = rows[
                    o * 8 : o * 8 + 8, h * 128 : (h + 1) * 128
                ]

    def rows_of(device_at, at, count):
        return pl.ds(pl.multiple_of(device_at * 48 + at, 16), count)

    def send(d, at, count):
        target = device(0, 0, d)
        pltpu.make_async_remote_copy(
            src_ref=msg.at[rows_of(target[2], at, count)],
            dst_ref=recv.at[rows_of(gz, at, count)],
            send_sem=row_send.at[0], recv_sem=row_recv.at[0],
            device_id=target, device_id_type=MESH,
        ).start()

    put(0, inner_rows)
    learn(1)
    for d in (1, -1, 2, -2, 3, -3):
        send(d, 0, 16)

    def when(flag, value, other):
        return jnp.where(jnp.full((1, 128), flag), value, other)

    label = [
        [
            when(inside[0], slots[0][1] + 1.0, 0.0),
            when(inside[1], slots[1][2] + 9.0, 0.0),
        ],
        [
            jnp.where(
                y_high,
                when(inside[3], slots[x][4] + 9.0, 0.0),
                when(inside[2], slots[x][3] + 1.0, 0.0),
            )
            for x in range(2)
        ],
        [
            jnp.where(
                z_at == 0,
                when(inside[4], slots[x][5] + 1.0, 0.0),
                jnp.where(z_at == 3, when(inside[5], slots[x][6] + 9.0, 0.0), 0.0),
            )
            for x in range(2)
        ],
    ]
    row, lane_all = iota((128, 128), 0), iota((128, 128), 1)
    once = ((lane_all & 7) == 0) & (lane_all < 64)
    which, who = [], []
    for x in range(2):
        value = jnp.where(
            row < 4, label[0][x], jnp.where(row < 8, label[1][x], jnp.where(row < 12, label[2][x], 0.0))
        )
        value = jnp.where(once & ((row & 3).astype(F32) == place[x]), value, 0.0)
        which.append(value.astype(BF16))
        row_o = iota((64, 128), 0)
        who.append((((row_o & 7) == 4) & ((row_o >> 3).astype(F32) == owner[x])).astype(BF16))
    labels = lax.dot_general(
        jnp.concatenate(who, axis=1), jnp.concatenate(which, axis=1),
        (((1,), (1,)), ((), ())), preferred_element_type=F32,
    )

    edge_codes = [
        code[0],
        code[1],
        jnp.where(y_high, pltpu.roll(code[1], 32, 1), code[0]) + 4.0,
        jnp.where(y_high, code[1], pltpu.roll(code[0], 96, 1)) + 4.0,
    ]
    edge_codes = [when(inside[i], edge_codes[i], -1.0) for i in range(4)]
    z_code = jnp.full((1, 128), -1.0, F32)
    for side in range(2):
        for x in range(2):
            for y in range(2):
                to, at = side * 4 + x * 2 + y, y * 4 + side * 3
                turn = (8 * (to - at)) % 128
                value = pltpu.roll(code[x], turn, 1) if turn else code[x]
                z_code = jnp.where(element == to, when(inside[4 + side], value, -1.0), z_code)

    for face in range(6):
        pl.when(inside[face])(functools.partial(halo_wait, face))

    def halo_rhs(i):
        return stacked(columns_of(slabs[i]))

    def rows_y(k, y):
        return jnp.concatenate([yv[k, x, y * 64 : y * 64 + 64] for x in range(2)], axis=0)

    def rows_z(k, z):
        return [
            yv[k, x, y * 64 + z * 16 : y * 64 + z * 16 + 16] for x in range(2) for y in range(2)
        ]

    sides = [yv[1, 0], yv[2, 1], rows_y(3, 0), rows_y(4, 1)]
    edges = sum(
        dot(selection(edge_codes[i]), terms(sides[i], halo_rhs(2 + i), own)) for i in range(4)
    )
    put(16, edges)
    ends = jnp.concatenate(rows_z(5, 0) + rows_z(6, 3), axis=0)
    edges = dot(selection(z_code), terms(ends, halo_rhs(6), own))
    put(32, jnp.concatenate([edges[:, :128] + labels, edges[:, 128:]], axis=1))

    learn(2)
    for d in (1, -1, 2, -2, 3, -3):
        send(d, 16, 32)
    send(4, 0, 48)
    stay = pltpu.make_async_copy(
        msg.at[rows_of(gz, 0, 48)], recv.at[rows_of(gz, 0, 48)], local_sem.at[0]
    )
    stay.start()

    others = pltpu.make_async_remote_copy(
        src_ref=msg.at[pl.ds(0, 336)], dst_ref=recv.at[pl.ds(0, 336)],
        send_sem=row_send.at[0], recv_sem=row_recv.at[0],
        device_id=device(0, 0, 1), device_id_type=MESH,
    )
    others.wait_send()
    others.wait_recv()
    stay.wait()


def spread(recv, out_ref):
    def came(stage, h, r):
        return recv[pl.ds(stage * 16 + h * 8 + r, 8, stride=48), :]

    for s in range(AGGS):
        for h in range(2):
            out_ref[:, s * 256 + h * 128 : s * 256 + h * 128 + 128] = came(0, h, s)
    marks = came(2, 0, 4)
    for axis in range(3):
        stage, at = (1, axis * 4) if axis < 2 else (2, 0)
        values = [[came(stage, h, at + p) for h in range(2)] for p in range(4)]
        tags = [
            jnp.broadcast_to(marks[:, axis * 4 + p : axis * 4 + p + 1], (8, 128)) for p in range(4)
        ]
        for column in range(16):
            hits = [tag == column + 1.0 for tag in tags]
            for h in range(2):
                total = jnp.where(hits[0], values[0][h], 0.0)
                for p in range(1, 4):
                    total += jnp.where(hits[p], values[p][h], 0.0)
                at_lane = (AGGS * (1 + 2 * axis) + column) * 256 + h * 128
                out_ref[:, at_lane : at_lane + 128] = total


def solution(mesh):
    sizes = (mesh.shape["gx"], mesh.shape["gy"], mesh.shape["gz"])

    def shards(fine_blocks, prolong, agg_map, owner_map):
        fine = fine_blocks.transpose(0, 1, 3, 2, 4).reshape(2, 2, 7, 4, 32, 128)
        fine = fine.transpose(0, 1, 2, 4, 3, 5).reshape(3584, 128)
        base = prolong.reshape(2, 2, 4, 8, 128).transpose(0, 1, 3, 2, 4)
        fine, base, agg_map, owner_map = (
            pltpu.with_memory_space_constraint(value, pltpu.HBM)
            for value in (fine, base, agg_map, owner_map)
        )
        rows = pl.pallas_call(
            functools.partial(kernel, sizes),
            out_shape=jax.ShapeDtypeStruct((384, 128), F32),
            in_specs=[pl.BlockSpec(memory_space=pltpu.HBM)] * 4,
            out_specs=pl.BlockSpec(memory_space=pltpu.VMEM),
            scratch_shapes=[
                pltpu.VMEM((3584, 128), F32),
                pltpu.VMEM((7, 8, 8, 128), F32),
                pltpu.VMEM((4,) + agg_map.shape[1:], jnp.int32),
                pltpu.VMEM((1, 1, AGGS), jnp.int32),
                pltpu.VMEM((FACES, 2, 128, 128), F32),
                pltpu.VMEM((384, 128), F32),
                pltpu.SemaphoreType.DMA((4,)),
                pltpu.SemaphoreType.DMA((6,)),
                pltpu.SemaphoreType.DMA((6,)),
                pltpu.SemaphoreType.DMA((1,)),
                pltpu.SemaphoreType.DMA((1,)),
                pltpu.SemaphoreType.REGULAR((3,)),
            ],
            compiler_params=pltpu.CompilerParams(
                collective_id=0, has_side_effects=True, vmem_limit_bytes=16 << 20
            ),
        )(fine, base, agg_map, owner_map)
        result = pl.pallas_call(
            spread,
            out_shape=jax.ShapeDtypeStruct((AGGS, 7 * AGGS * 256), F32),
            in_specs=[pl.BlockSpec(memory_space=pltpu.VMEM)],
            out_specs=pl.BlockSpec(memory_space=pltpu.VMEM),
            compiler_params=pltpu.CompilerParams(vmem_limit_bytes=8 << 20),
        )(rows)
        return result.reshape(1, 1, AGGS, 7 * AGGS * 256)

    placed = (P("gx", "gy", "gz", None, None), P("gx", "gy", "gz", None), P(), P("gx", "gy", "gz"))
    return jax.shard_map(
        shards, mesh=mesh, in_specs=placed, out_specs=P("gx", "gy", "gz", None), check_vma=False
    )
```

time: 25.8 us -> 22.3 us (0.86)
  Pallas kernels: 25.6 us -> 22.1 us
    pallas_call x1, Pallas kernels: 23.7 us -> 21.1 us  [shards(): pl.pallas_call(functools.partial(kernel, sizes), out_shape=jax.ShapeDtype...]
    pallas_call x1, Pallas kernels: 1.9 us -> 0.97 us  [shards(): pl.pallas_call(spread, out_shape=jax.ShapeDtypeStruct((AGGS, 7 * AGGS * 2...]
where the time goes in v3:
time: 22.3 us; the launch traced here: 22.1 us
  Pallas kernels  22.1 us (99%)
    pallas_call x1, Pallas kernels, shards(): pl.pallas_call(functools.partial(kernel, sizes), out_shape=jax.ShapeDtype...  21.1 us
    pallas_call x1, Pallas kernels, shards(): pl.pallas_call(spread, out_shape=jax.ShapeDtypeStruct((AGGS, 7 * AGGS * 2...  0.97 us

profile of v3, /device:TPU:8, one launch (start us, length us, event | category | flops | bytes accessed | tf_op | source)
XLA Modules:
  0.0 22.1 jit_solution(6406011680803232133)
XLA Ops:
  0.0 21.1 %shard_map.46.recv = f32[384,128]{1,0:T(8,128)S(1)} custom-call(f32[3584,128]{1,0:T(8,128)} %bitcast.11, f32[2,2,8,4,128]{4,3,2,1,0:T(4,128)} %bitcast.12, s32[16,24,32]{2,1,0:T(8,128)} %agg_hbm.1, s32[1,1,8]{2,1,0:T(1,128)} %own_hbm.1), custom_call_target="tpu_custom_call" | custom-call | tf_op jit(solution)/shard_map/pallas_call | solution.py:443
  21.1 1.0 %shard_map.47 = f32[8,14336]{1,0:T(8,128)} custom-call(f32[384,128]{1,0:T(8,128)S(1)} %shard_map.46.recv), custom_call_target="tpu_custom_call" | custom-call | tf_op jit(solution)/shard_map/pallas_call | solution.py:466

commit v4 on v3

--- a/solution.py
+++ b/solution.py
@@ -65,13 +65,6 @@
         pl.semaphore_signal(sem, inc=1, device_id=target, device_id_type=MESH)
 
     inside = (gx > 0, gx < nx - 1, gy > 0, gy < ny - 1, gz > 0, gz < nz - 1)
-
-    barrier = pltpu.get_barrier_semaphore()
-    for n, step in enumerate(STEPS[1:]):
-        if n < 4:
-            pl.when(inside[n])(functools.partial(signal, barrier, device(*step)))
-        else:
-            signal(barrier, device(*step))
 
     def copied(dst, n):
         return pltpu.make_async_copy(dst, dst, local_sem.at[n])
@@ -92,6 +85,13 @@
         ).start()
     pltpu.make_async_copy(own_hbm, own_v, local_sem.at[3]).start()
 
+    barrier = pltpu.get_barrier_semaphore()
+    for n, step in enumerate(STEPS[1:]):
+        if n < 4:
+            pl.when(inside[n])(functools.partial(signal, barrier, device(*step)))
+        else:
+            signal(barrier, device(*step))
+
     halo = [[] for _ in range(6)]
 
     def halo_copy(face, src, dst):
@@ -123,14 +123,21 @@
         done.wait_send()
         done.wait_recv()
 
-    def tell(stage):
-        for step in (-1, 1):
-            signal(ready.at[stage], device(0, 0, step))
-
-    def learn(stage):
-        pl.semaphore_wait(ready.at[stage], 2)
-        if stage < 2:
-            tell(stage + 1)
+    past = {1: lax.rem(nz - gz, nz), -1: gz}
+    ways = ((0, 1), (1, -1))
+
+    def late(way, d):
+        return (past[way] >= 1) & (past[way] <= d)
+
+    def learn(stage, last):
+        for n, way in ways:
+            flag = late(way, stage + 2)
+
+            @pl.when(flag if last else ~flag)
+            def _():
+                pl.semaphore_wait(ready.at[n, stage], 1)
+                if stage < 2:
+                    signal(ready.at[n, stage + 1], device(0, 0, -way))
 
     def meet():
         pl.semaphore_wait(barrier, 2 + sum(flag.astype(jnp.int32) for flag in inside[:4]))
@@ -141,7 +148,8 @@
                 for copy in halo[face]:
                     copy.start()
 
-        tell(0)
+        for n, way in ways:
+            signal(ready.at[n, 0], device(0, 0, -way))
         for face in range(4):
 
             @pl.when(~inside[face])
@@ -153,6 +161,8 @@
             @pl.when(~inside[face])
             def _():
                 slabs[6, :, (face - 4) * 4 : (face - 4) * 4 + 4, :] = jnp.zeros((8, 4, 128), F32)
+
+    meet()
 
     copied(slabs.at[pl.ds(0, 2)], 0).wait()
     own_cols = [columns_of(slabs[x]) for x in range(2)]
@@ -172,9 +182,8 @@
                 parts.append(jnp.concatenate([rows[:, :128], rows[:, 128:]], axis=0))
             left[x, y] = parts
 
-    meet()
-
     low_lanes = iota((64, 128), 1) < 64
+    learn(0, False)
     copied(a_v, 1).wait()
     for x in range(2):
         for y in range(2):
@@ -191,7 +200,7 @@
                 tile = both[:, k * 128 : (k + 1) * 128]
                 tile = jnp.where(low_lanes, tile[0:64] + tile[128:192], tile[64:128] + tile[192:256])
                 yv[k, x, y * 64 : y * 64 + 64, :] = tile + pltpu.roll(tile, 64, 1)
-    learn(0)
+    learn(1, False)
 
     copied(agg_v, 2).wait()
     copied(own_v, 3).wait()
@@ -235,56 +244,67 @@
     fold = ((iota((256, 128), 0) & 15) == (iota((256, 128), 1) & 15)).astype(BF16)
     group = iota((16, 128), 1) >> 4
 
-    def terms(lhs, rhs, partners, places=tuple(range(8))):
-        count = len(partners)
-        block = dot(jnp.concatenate(split(lhs), axis=1), rhs)
-        block = jnp.concatenate(
-            [
-                jnp.where(group == partner, block[i * 16 : i * 16 + 16], 0.0)
-                for i, partner in enumerate(partners)
-            ],
-            axis=0,
-        )
-        tall = dot(jnp.concatenate(split(block), axis=1), fold).reshape(count * 2, 8, 128)
+    def picked(block, partners):
+        return [
+            jnp.where(group == partner, block[i * 16 : i * 16 + 16], 0.0)
+            for i, partner in enumerate(partners)
+        ]
+
+    def flat(parts):
+        count = len(parts)
+        tall = dot(jnp.concatenate(split(jnp.concatenate(parts, axis=0)), axis=1), fold)
+        tall = tall.reshape(count * 2, 8, 128)
         on_c = iota((count * 2, 8, 128), 1) == (iota((count * 2, 8, 128), 2) >> 4)
         tall = jnp.where(on_c, tall, 0.0).reshape(count, 2, 8, 128)
-        rows = [jnp.zeros((8, 256), F32)] * 8
-        for i, at in enumerate(places):
-            rows[at] = jnp.concatenate([tall[i, 0], tall[i, 1]], axis=1)
-        return jnp.concatenate(split(jnp.concatenate(rows, axis=0)), axis=0)
+        return [jnp.concatenate([tall[i, 0], tall[i, 1]], axis=1) for i in range(count)]
+
+    def summed(codes, rows):
+        factors = []
+        for i in range(len(codes)):
+            factors += split(jnp.concatenate(rows[i * 8 : i * 8 + 8], axis=0))
+        return dot(
+            jnp.concatenate([selection(code) for code in codes], axis=1),
+            jnp.concatenate(factors, axis=0),
+        )
+
+    def wide(value):
+        return jnp.concatenate(split(value), axis=1)
 
     own = tuple(range(8))
     z_odd = (z_at & 1) == 1
-    inner_rows = jnp.zeros((64, 256), F32)
+    none = jnp.zeros((8, 256), F32)
+    parts, codes = [], []
     for x in range(2):
         y = [yv[k, x] for k in range(FACES)]
         at = [[y[k][e * 16 : e * 16 + 16] for e in range(8)] for k in (5, 6)]
-        cross = 2 - x
-        tiles = [
-            (y[0], own_rhs[x], own, own, slots[x][0]),
-            (y[cross], own_rhs[1 - x], own, own, slots[x][cross]),
-            (
-                jnp.concatenate([y[4][:64], y[3][64:]], axis=0), own_rhs[x],
-                tuple(e ^ 4 for e in own), own, jnp.where(y_high, slots[x][3], slots[x][4]),
-            ),
-            (
-                jnp.concatenate([at[1 - (e & 1)][e] for e in own], axis=0), own_rhs[x],
-                tuple(e ^ 1 for e in own), own, jnp.where(z_odd, slots[x][5], slots[x][6]),
-            ),
-            (
-                jnp.concatenate([at[e & 1][e] for e in (1, 2, 5, 6)], axis=0), own_rhs[x],
-                (2, 1, 6, 5), (1, 2, 5, 6),
-                jnp.where(
-                    z_at == 1, slots[x][6], jnp.where(z_at == 2, slots[x][5], -1000.0)
-                ),
-            ),
+        lhs = (
+            [y[0], yv[1 + x, 1 - x], y[4][:64], y[3][64:]]
+            + [at[1 - (e & 1)][e] for e in own]
+            + [at[e & 1][e] for e in (1, 2, 5, 6)]
+        )
+        partners = (
+            own + own + tuple(e ^ 4 for e in own) + tuple(e ^ 1 for e in own) + (2, 1, 6, 5)
+        )
+        parts += picked(dot(wide(jnp.concatenate(lhs, axis=0)), own_rhs[x]), partners)
+        other = 1 - x
+        codes += [
+            owner[x] * 8.0 + slots[x][0],
+            owner[other] * 8.0 + slots[other][2 - other],
+            owner[x] * 8.0 + jnp.where(y_high, slots[x][3], slots[x][4]),
+            owner[x] * 8.0 + jnp.where(z_odd, slots[x][5], slots[x][6]),
+            owner[x] * 8.0
+            + jnp.where(z_at == 1, slots[x][6], jnp.where(z_at == 2, slots[x][5], -1000.0)),
         ]
-        for lhs, rhs, partners, places, column in tiles:
-            inner_rows += dot(selection(owner[x] * 8.0 + column), terms(lhs, rhs, partners, places))
+    rows = flat(parts)
+    padded = []
+    for x in range(2):
+        part = rows[x * 36 : x * 36 + 36]
+        padded += part[:32] + [none, part[32], part[33], none, none, part[34], part[35], none]
+    inner_rows = summed(codes, padded)
 
     def put(at, rows):
         for o in range(AGGS):
-            for h in range(2):
+            for h in range(rows.shape[1] // 128):
                 msg[pl.ds(o * 48 + at + h * 8, 8), :] = rows[
                     o * 8 : o * 8 + 8, h * 128 : (h + 1) * 128
                 ]
@@ -301,10 +321,18 @@
             device_id=target, device_id_type=MESH,
         ).start()
 
+    later = {d: late(1 if d > 0 else -1, abs(d)) for d in (2, -2, 3, -3)}
+    later[4] = jnp.where(gz < nz // 2, late(1, 4), late(-1, 4))
+
+    def send_all(at, count):
+        for d in (1, -1):
+            send(d, at, count)
+        for d in later:
+            pl.when(~later[d])(functools.partial(send, d, at, count))
+
     put(0, inner_rows)
-    learn(1)
-    for d in (1, -1, 2, -2, 3, -3):
-        send(d, 0, 16)
+    learn(2, False)
+    send_all(0, 16)
 
     def when(flag, value, other):
         return jnp.where(jnp.full((1, 128), flag), value, other)
@@ -340,8 +368,7 @@
         )
         value = jnp.where(once & ((row & 3).astype(F32) == place[x]), value, 0.0)
         which.append(value.astype(BF16))
-        row_o = iota((64, 128), 0)
-        who.append((((row_o & 7) == 4) & ((row_o >> 3).astype(F32) == owner[x])).astype(BF16))
+        who.append((iota((8, 128), 0).astype(F32) == owner[x]).astype(BF16))
     labels = lax.dot_general(
         jnp.concatenate(who, axis=1), jnp.concatenate(which, axis=1),
         (((1,), (1,)), ((), ())), preferred_element_type=F32,
@@ -377,26 +404,30 @@
             yv[k, x, y * 64 + z * 16 : y * 64 + z * 16 + 16] for x in range(2) for y in range(2)
         ]
 
-    sides = [yv[1, 0], yv[2, 1], rows_y(3, 0), rows_y(4, 1)]
-    edges = sum(
-        dot(selection(edge_codes[i]), terms(sides[i], halo_rhs(2 + i), own)) for i in range(4)
-    )
-    put(16, edges)
     ends = jnp.concatenate(rows_z(5, 0) + rows_z(6, 3), axis=0)
-    edges = dot(selection(z_code), terms(ends, halo_rhs(6), own))
-    put(32, jnp.concatenate([edges[:, :128] + labels, edges[:, 128:]], axis=1))
-
-    learn(2)
-    for d in (1, -1, 2, -2, 3, -3):
-        send(d, 16, 32)
-    send(4, 0, 48)
+    sides = [yv[1, 0], yv[2, 1], rows_y(3, 0), rows_y(4, 1), ends]
+    parts = []
+    for i in range(5):
+        parts += picked(dot(wide(sides[i]), halo_rhs(2 + i)), own)
+    rows = flat(parts)
+    put(16, summed(edge_codes, rows[:32]))
+    edges = summed([z_code], rows[32:])
+    put(32, edges[:, :128] + pltpu.roll(edges[:, 128:], 4, 0))
+    for o in range(AGGS):
+        msg[pl.ds(o * 48 + 40, 1), :] = labels[o : o + 1]
+
+    send_all(16, 25)
     stay = pltpu.make_async_copy(
-        msg.at[rows_of(gz, 0, 48)], recv.at[rows_of(gz, 0, 48)], local_sem.at[0]
+        msg.at[rows_of(gz, 0, 41)], recv.at[rows_of(gz, 0, 41)], local_sem.at[0]
     )
     stay.start()
+    for stage in range(3):
+        learn(stage, True)
+        for d in (stage + 2, -stage - 2) if stage < 2 else (4,):
+            pl.when(later[d])(functools.partial(send, d, 0, 41))
 
     others = pltpu.make_async_remote_copy(
-        src_ref=msg.at[pl.ds(0, 336)], dst_ref=recv.at[pl.ds(0, 336)],
+        src_ref=msg.at[pl.ds(0, 287)], dst_ref=recv.at[pl.ds(0, 287)],
         send_sem=row_send.at[0], recv_sem=row_recv.at[0],
         device_id=device(0, 0, 1), device_id_type=MESH,
     )
@@ -406,16 +437,16 @@
 
 
 def spread(recv, out_ref):
-    def came(stage, h, r):
-        return recv[pl.ds(stage * 16 + h * 8 + r, 8, stride=48), :]
+    def came(row):
+        return recv[pl.ds(row, 8, stride=48), :]
 
     for s in range(AGGS):
         for h in range(2):
-            out_ref[:, s * 256 + h * 128 : s * 256 + h * 128 + 128] = came(0, h, s)
-    marks = came(2, 0, 4)
+            out_ref[:, s * 256 + h * 128 : s * 256 + h * 128 + 128] = came(h * 8 + s)
+    marks = came(40)
     for axis in range(3):
-        stage, at = (1, axis * 4) if axis < 2 else (2, 0)
-        values = [[came(stage, h, at + p) for h in range(2)] for p in range(4)]
+        first, step = (16 + axis * 4, 8) if axis < 2 else (32, 4)
+        values = [[came(first + h * step + p) for h in range(2)] for p in range(4)]
         tags = [
             jnp.broadcast_to(marks[:, axis * 4 + p : axis * 4 + p + 1], (8, 128)) for p in range(4)
         ]
@@ -457,7 +488,7 @@
                 pltpu.SemaphoreType.DMA((6,)),
                 pltpu.SemaphoreType.DMA((1,)),
                 pltpu.SemaphoreType.DMA((1,)),
-                pltpu.SemaphoreType.REGULAR((3,)),
+                pltpu.SemaphoreType.REGULAR((2, 3)),
             ],
             compiler_params=pltpu.CompilerParams(
                 collective_id=0, has_side_effects=True, vmem_limit_bytes=16 << 20

time: 22.3 us -> 20.9 us (0.937)
  Pallas kernels: 22.1 us -> 20.7 us
    pallas_call x1, Pallas kernels: 21.1 us -> 19.8 us  [shards(): pl.pallas_call(functools.partial(kernel, sizes), out_shape=jax.ShapeDtype...]
where the time goes in v4:
time: 20.9 us; the launch traced here: 20.7 us
  Pallas kernels  20.7 us (99%)
    pallas_call x1, Pallas kernels, shards(): pl.pallas_call(functools.partial(kernel, sizes), out_shape=jax.ShapeDtype...  19.8 us
    pallas_call x1, Pallas kernels, shards(): pl.pallas_call(spread, out_shape=jax.ShapeDtypeStruct((AGGS, 7 * AGGS * 2...  0.97 us

profile of v4, /device:TPU:8, one launch (start us, length us, event | category | flops | bytes accessed | tf_op | source)
XLA Modules:
  0.0 20.7 jit_solution(13717554174213049608)
XLA Ops:
  0.0 19.8 %shard_map.46.recv = f32[384,128]{1,0:T(8,128)S(1)} custom-call(f32[3584,128]{1,0:T(8,128)} %bitcast.11, f32[2,2,8,4,128]{4,3,2,1,0:T(4,128)} %bitcast.12, s32[16,24,32]{2,1,0:T(8,128)} %agg_hbm.1, s32[1,1,8]{2,1,0:T(1,128)} %own_hbm.1), custom_call_target="tpu_custom_call" | custom-call | tf_op jit(solution)/shard_map/pallas_call | solution.py:474
  19.8 1.0 %shard_map.47 = f32[8,14336]{1,0:T(8,128)} custom-call(f32[384,128]{1,0:T(8,128)S(1)} %shard_map.46.recv), custom_call_target="tpu_custom_call" | custom-call | tf_op jit(solution)/shard_map/pallas_call | solution.py:497

commit v5 on v4

--- a/solution.py
+++ b/solution.py
@@ -48,7 +48,7 @@
 
 def kernel(
     sizes, a_hbm, p_hbm, agg_hbm, own_hbm, recv,
-    a_v, slabs, agg_v, own_v, yv, msg,
+    a_v, slabs, faces, sides_in, agg_v, own_v, yv, msg,
     local_sem, halo_send, halo_recv, row_send, row_recv, ready,
 ):
     nx, ny, nz = sizes
@@ -103,18 +103,15 @@
             )
         )
 
+    for face in range(4):
+        halo_copy(face, faces.at[face], sides_in.at[face ^ 1])
     for u in range(2):
-        half = pl.ds(4 * u, 4)
-        halo_copy(0, p_hbm.at[0, u], slabs.at[3, :, half, :])
-        halo_copy(1, p_hbm.at[1, u], slabs.at[2, :, half, :])
-        halo_copy(2, p_hbm.at[u, 0], slabs.at[5, :, half, :])
-        halo_copy(3, p_hbm.at[u, 1], slabs.at[4, :, half, :])
         for v in range(2):
-            halo_copy(4, p_hbm.at[u, v, :, 0, :], slabs.at[6, :, 4 + u * 2 + v, :])
-            halo_copy(5, p_hbm.at[u, v, :, 3, :], slabs.at[6, :, u * 2 + v, :])
+            halo_copy(4, p_hbm.at[u, v, :, 0, :], slabs.at[2, :, 4 + u * 2 + v, :])
+            halo_copy(5, p_hbm.at[u, v, :, 3, :], slabs.at[2, :, u * 2 + v, :])
 
     def halo_wait(face):
-        slab = slabs.at[2 + face] if face < 4 else slabs.at[6, :, pl.ds((face - 4) * 4, 4), :]
+        slab = sides_in.at[face] if face < 4 else slabs.at[2, :, pl.ds((face - 4) * 4, 4), :]
         done = pltpu.make_async_remote_copy(
             src_ref=slab, dst_ref=slab,
             send_sem=halo_send.at[face], recv_sem=halo_recv.at[face ^ 1],
@@ -139,34 +136,42 @@
                 if stage < 2:
                     signal(ready.at[n, stage + 1], device(0, 0, -way))
 
-    def meet():
-        pl.semaphore_wait(barrier, 2 + sum(flag.astype(jnp.int32) for flag in inside[:4]))
-        for face in (2, 3, 4, 5, 0, 1):
+    def send_faces(which):
+        for face in which:
 
             @pl.when(inside[face])
             def _():
                 for copy in halo[face]:
                     copy.start()
 
+    def meet():
+        pl.semaphore_wait(barrier, 2 + sum(flag.astype(jnp.int32) for flag in inside[:4]))
+        send_faces((4, 5))
+
         for n, way in ways:
             signal(ready.at[n, 0], device(0, 0, -way))
         for face in range(4):
 
             @pl.when(~inside[face])
             def _():
-                slabs[2 + face] = jnp.zeros((8, 8, 128), F32)
+                sides_in[face] = jnp.zeros((64, 128), F32)
 
         for face in (4, 5):
 
             @pl.when(~inside[face])
             def _():
-                slabs[6, :, (face - 4) * 4 : (face - 4) * 4 + 4, :] = jnp.zeros((8, 4, 128), F32)
+                slabs[2, :, (face - 4) * 4 : (face - 4) * 4 + 4, :] = jnp.zeros((8, 4, 128), F32)
 
     meet()
 
     copied(slabs.at[pl.ds(0, 2)], 0).wait()
     own_cols = [columns_of(slabs[x]) for x in range(2)]
     own_rhs = [stacked(cols) for cols in own_cols]
+    low_lanes = iota((64, 128), 1) < 64
+    for x in range(2):
+        faces[x] = own_cols[x]
+    faces[2] = jnp.where(low_lanes, own_cols[0], pltpu.roll(own_cols[1], 64, 1))
+    faces[3] = jnp.where(low_lanes, pltpu.roll(own_cols[0], 64, 1), own_cols[1])
     turned = jnp.concatenate(split(jnp.concatenate(own_cols, axis=0).T), axis=0)
     lane = iota((128, 256), 1)
     spot = 2 * ((lane & 127) >> 2) + (lane >> 7)
@@ -182,7 +187,8 @@
                 parts.append(jnp.concatenate([rows[:, :128], rows[:, 128:]], axis=0))
             left[x, y] = parts
 
-    low_lanes = iota((64, 128), 1) < 64
+    send_faces((2, 3, 0, 1))
+
     learn(0, False)
     copied(a_v, 1).wait()
     for x in range(2):
@@ -393,8 +399,8 @@
     for face in range(6):
         pl.when(inside[face])(functools.partial(halo_wait, face))
 
-    def halo_rhs(i):
-        return stacked(columns_of(slabs[i]))
+    def halo_rhs(face):
+        return stacked(sides_in[face] if face < 4 else columns_of(slabs[2]))
 
     def rows_y(k, y):
         return jnp.concatenate([yv[k, x, y * 64 : y * 64 + 64] for x in range(2)], axis=0)
@@ -408,7 +414,7 @@
     sides = [yv[1, 0], yv[2, 1], rows_y(3, 0), rows_y(4, 1), ends]
     parts = []
     for i in range(5):
-        parts += picked(dot(wide(sides[i]), halo_rhs(2 + i)), own)
+        parts += picked(dot(wide(sides[i]), halo_rhs(i)), own)
     rows = flat(parts)
     put(16, summed(edge_codes, rows[:32]))
     edges = summed([z_code], rows[32:])
@@ -436,13 +442,23 @@
     stay.wait()
 
 
-def spread(recv, out_ref):
+def spread(recv, out_hbm, out_ref, sem):
+    pieces = []
+
+    def write(start, lanes):
+        piece = (slice(None), pl.ds(start, lanes))
+        pieces.append(
+            pltpu.make_async_copy(out_ref.at[piece], out_hbm.at[piece], sem.at[len(pieces)])
+        )
+        pieces[-1].start()
+
     def came(row):
         return recv[pl.ds(row, 8, stride=48), :]
 
     for s in range(AGGS):
         for h in range(2):
             out_ref[:, s * 256 + h * 128 : s * 256 + h * 128 + 128] = came(h * 8 + s)
+    write(0, AGGS * 256)
     marks = came(40)
     for axis in range(3):
         first, step = (16 + axis * 4, 8) if axis < 2 else (32, 4)
@@ -458,6 +474,9 @@
                     total += jnp.where(hits[p], values[p][h], 0.0)
                 at_lane = (AGGS * (1 + 2 * axis) + column) * 256 + h * 128
                 out_ref[:, at_lane : at_lane + 128] = total
+        write(AGGS * (1 + 2 * axis) * 256, AGGS * 512)
+    for piece in pieces:
+        piece.wait()
 
 
 def solution(mesh):
@@ -478,7 +497,9 @@
             out_specs=pl.BlockSpec(memory_space=pltpu.VMEM),
             scratch_shapes=[
                 pltpu.VMEM((3584, 128), F32),
-                pltpu.VMEM((7, 8, 8, 128), F32),
+                pltpu.VMEM((3, 8, 8, 128), F32),
+                pltpu.VMEM((4, 64, 128), F32),
+                pltpu.VMEM((4, 64, 128), F32),
                 pltpu.VMEM((4,) + agg_map.shape[1:], jnp.int32),
                 pltpu.VMEM((1, 1, AGGS), jnp.int32),
                 pltpu.VMEM((FACES, 2, 128, 128), F32),
@@ -498,7 +519,11 @@
             spread,
             out_shape=jax.ShapeDtypeStruct((AGGS, 7 * AGGS * 256), F32),
             in_specs=[pl.BlockSpec(memory_space=pltpu.VMEM)],
-            out_specs=pl.BlockSpec(memory_space=pltpu.VMEM),
+            out_specs=pl.BlockSpec(memory_space=pltpu.HBM),
+            scratch_shapes=[
+                pltpu.VMEM((AGGS, 7 * AGGS * 256), F32),
+                pltpu.SemaphoreType.DMA((4,)),
+            ],
             compiler_params=pltpu.CompilerParams(vmem_limit_bytes=8 << 20),
         )(rows)
         return result.reshape(1, 1, AGGS, 7 * AGGS * 256)

time: 20.9 us -> 20.6 us (0.986)
  Pallas kernels: 20.7 us -> 20.4 us
    pallas_call x1, Pallas kernels: 19.8 us -> 19.5 us  [shards(): pl.pallas_call(functools.partial(kernel, sizes), out_shape=jax.ShapeDtype...]
where the time goes in v5:
time: 20.6 us; the launch traced here: 20.4 us
  Pallas kernels  20.4 us (99%)
    pallas_call x1, Pallas kernels, shards(): pl.pallas_call(functools.partial(kernel, sizes), out_shape=jax.ShapeDtype...  19.5 us
    pallas_call x1, Pallas kernels, shards(): pl.pallas_call(spread, out_shape=jax.ShapeDtypeStruct((AGGS, 7 * AGGS * 2...  0.93 us

profile of v5, /device:TPU:8, one launch (start us, length us, event | category | flops | bytes accessed | tf_op | source)
XLA Modules:
  0.0 20.4 jit_solution(9305660487465632328)
XLA Ops:
  0.0 19.5 %shard_map.46.recv = f32[384,128]{1,0:T(8,128)S(1)} custom-call(f32[3584,128]{1,0:T(8,128)} %bitcast.11, f32[2,2,8,4,128]{4,3,2,1,0:T(4,128)} %bitcast.12, s32[16,24,32]{2,1,0:T(8,128)} %agg_hbm.1, s32[1,1,8]{2,1,0:T(1,128)} %own_hbm.1), custom_call_target="tpu_custom_call" | custom-call | tf_op jit(solution)/shard_map/pallas_call | solution.py:493
  19.5 0.9 %shard_map.47 = f32[8,14336]{1,0:T(8,128)} custom-call(f32[384,128]{1,0:T(8,128)S(1)} %shard_map.46.recv), custom_call_target="tpu_custom_call" | custom-call | tf_op jit(solution)/shard_map/pallas_call | solution.py:518

commit v6 on v5

--- a/solution.py
+++ b/solution.py
@@ -301,12 +301,11 @@
             owner[x] * 8.0
             + jnp.where(z_at == 1, slots[x][6], jnp.where(z_at == 2, slots[x][5], -1000.0)),
         ]
-    rows = flat(parts)
-    padded = []
-    for x in range(2):
-        part = rows[x * 36 : x * 36 + 36]
-        padded += part[:32] + [none, part[32], part[33], none, none, part[34], part[35], none]
-    inner_rows = summed(codes, padded)
+    inner_rows = jnp.zeros((64, 256), F32)
+    for x in range(2):
+        part = flat(parts[x * 36 : x * 36 + 36])
+        padded = part[:32] + [none, part[32], part[33], none, none, part[34], part[35], none]
+        inner_rows += summed(codes[x * 5 : x * 5 + 5], padded)
 
     def put(at, rows):
         for o in range(AGGS):

time: 20.6 us -> 20.5 us (level)
  no operation moved by 1% of the time
where the time goes in v6:
time: 20.5 us; the launch traced here: 20.3 us
  Pallas kernels  20.3 us (99%)
    pallas_call x1, Pallas kernels, shards(): pl.pallas_call(functools.partial(kernel, sizes), out_shape=jax.ShapeDtype...  19.4 us
    pallas_call x1, Pallas kernels, shards(): pl.pallas_call(spread, out_shape=jax.ShapeDtypeStruct((AGGS, 7 * AGGS * 2...  0.93 us

profile of v6, /device:TPU:8, one launch (start us, length us, event | category | flops | bytes accessed | tf_op | source)
XLA Modules:
  0.0 20.3 jit_solution(11666308766228475580)
XLA Ops:
  0.0 19.4 %shard_map.46.recv = f32[384,128]{1,0:T(8,128)S(1)} custom-call(f32[3584,128]{1,0:T(8,128)} %bitcast.11, f32[2,2,8,4,128]{4,3,2,1,0:T(4,128)} %bitcast.12, s32[16,24,32]{2,1,0:T(8,128)} %agg_hbm.1, s32[1,1,8]{2,1,0:T(1,128)} %own_hbm.1), custom_call_target="tpu_custom_call" | custom-call | tf_op jit(solution)/shard_map/pallas_call | solution.py:492
  19.4 0.9 %shard_map.47 = f32[8,14336]{1,0:T(8,128)} custom-call(f32[384,128]{1,0:T(8,128)S(1)} %shard_map.46.recv), custom_call_target="tpu_custom_call" | custom-call | tf_op jit(solution)/shard_map/pallas_call | solution.py:517
